TPU v7x, 512 devices: a whole 4x8x8 slice. The times are simulated.
512 devices in a mesh: blk: 16 (over x, z_lo, core), dp: 32 (over z_hi, y).
Axes of the slice: x: 4, y: 8, z: 8 (z_hi: 4, z_lo: 2; z = z_hi * 2 + z_lo), core: 2. Of those that a mesh axis runs over, the one named last changes fastest.
Arguments:
- spikes: bfloat16 [4, 16384, 128], P(None, 'blk'), may hold values from 0 to 1, as said below
- rec_weights: bfloat16 [16384, 16384], P('blk', 'dp'), may hold values from -0.046875 to 0.046875
- in_current: float32 [4, 16384, 128], P(None, ('blk', 'dp')), may hold values from -6 to 6
- volt_init: float32 [16384, 128], P(('blk', 'dp')), may hold values from -6 to 6
- adapt_init: float32 [16384, 128], P(('blk', 'dp')), may hold values from 0 to 3
- mem_decay: float32 [16384], P(('blk', 'dp')), may hold values from 0.5 to 0.97
- adapt_decay: float32 [16384], P(('blk', 'dp')), may hold values from 0.7 to 0.99
- adapt_gain: float32 [16384], P(('blk', 'dp')), may hold values from 0.1 to 1
- resting_trigger_level: float32 [16384], P(('blk', 'dp')), may hold values from 0.5 to 1.5
- pulse_sensitivity: float32 [4, 16384, 128], P(None, ('blk', 'dp')), may hold values from -6 to 6
- volt_cot: float32 [16384, 128], P(('blk', 'dp')), may hold values from -6 to 6
- adapt_cot: float32 [16384, 128], P(('blk', 'dp')), may hold values from -6 to 6
Outputs:
- volt_adj: float32 [16384, 128], P(('blk', 'dp'))
- adapt_adj: float32 [16384, 128], P(('blk', 'dp'))
- weight_grad: float32 [16384, 16384], P('blk', 'dp')
Inputs may be any that keep to these rules, and one draw needn't show every extreme that they name: `spikes`: every entry is 0 or 1.
All inputs are finite; a program needn't handle non-finite values.
Results may differ from a plain program's by a relative error of at most 0.0024.
Values may be sent and summed in bfloat16 or wider, within the bound.
No kernel may reach another device: no remote copies, remote signals or barrier semaphores. Data moves between devices by JAX's collectives and lax.ppermute only.
A program may use at most 64 MiB of HBM per device.

v0:
```python
import jax
import jax.numpy as jnp
from jax import lax
from jax.sharding import PartitionSpec as P

pseudo_derivative_factor = 0.5


def cut_along(shard, dim, length):
    dims = shard.shape
    parts = shard.reshape(*dims[:dim], length, dims[dim] // length, *dims[dim + 1 :])
    return jnp.moveaxis(parts, dim, 0)


def summed_on_arrival(shard, axis, dim):
    length = lax.axis_size(axis)
    parts = lax.all_to_all(cut_along(shard, dim, length), axis, 0, 0, tiled=True)
    return jnp.sum(parts, axis=0)


def copy_for_each(shard, axis):
    copies = jnp.broadcast_to(shard, (lax.axis_size(axis), *shard.shape))
    return lax.all_to_all(copies, axis, split_axis=0, concat_axis=0, tiled=True)


def laid_out(parts, dim):
    dims = list(parts.shape[1:])
    dims[dim] *= parts.shape[0]
    return jnp.moveaxis(parts, 0, dim).reshape(dims)


def gather_directly(shard, axis, dim):
    parts = copy_for_each(shard, axis)
    return laid_out(parts, dim)


def window_terms(weights, fired_all):
    return jnp.einsum("pc,tpb->ctb", weights, fired_all, preferred_element_type=jnp.float32)


def row_terms(weights, pieces):
    return jnp.dot(weights, pieces, preferred_element_type=jnp.float32)


def body(
    spikes,
    rec_weights,
    in_current,
    volt_init,
    adapt_init,
    mem_decay,
    adapt_decay,
    adapt_gain,
    resting_trigger_level,
    pulse_sensitivity,
    volt_cot,
    adapt_cot,
):
    num_steps = spikes.shape[0]
    own_width = volt_init.shape[0]
    dp_index = lax.axis_index("dp")
    own_fired = lax.dynamic_slice_in_dim(spikes, dp_index * own_width, own_width, 1).astype(
        jnp.float32
    )
    leak_rate = mem_decay[:, None]
    keep_rate = adapt_decay[:, None]
    gain_col = adapt_gain[:, None]
    minimum_column = resting_trigger_level[:, None]
    window_totals = summed_on_arrival(window_terms(rec_weights, spikes), "blk", 0)
    voltage = volt_init
    adaptation = adapt_init
    threshold_values = []
    surrogates = []
    for moment in range(num_steps):
        current = window_totals[:, moment]
        thresh = minimum_column + gain_col * adaptation
        surrogate = pseudo_derivative_factor / jnp.square(1.0 + jnp.abs(voltage - thresh))
        fired = own_fired[moment]
        voltage = leak_rate * voltage + current + in_current[moment] - thresh * fired
        adaptation = keep_rate * adaptation + fired
        threshold_values.append(thresh)
        surrogates.append(surrogate)
    volt_adj = volt_cot
    adapt_adj = adapt_cot
    kept_pieces = []
    for moment in reversed(range(num_steps)):
        rounded = volt_adj.astype(jnp.bfloat16)
        pieces = gather_directly(rounded, "blk", 0)
        recurrent_matrix = summed_on_arrival(row_terms(rec_weights, pieces), "dp", 0)
        kept_pieces.insert(0, pieces)
        fired = own_fired[moment]
        spike_adj = (
            pulse_sensitivity[moment]
            + recurrent_matrix
            - threshold_values[moment] * volt_adj
            + adapt_adj
        )
        through = surrogates[moment] * spike_adj
        new_volt = leak_rate * volt_adj + through
        adapt_adj = keep_rate * adapt_adj - gain_col * (fired * volt_adj + through)
        volt_adj = new_volt
    weight_sum = jnp.einsum(
        "tpb,tcb->pc", spikes, jnp.stack(kept_pieces), preferred_element_type=jnp.float32
    )
    return (volt_adj, adapt_adj, weight_sum)


def solution(mesh):
    return jax.shard_map(
        body,
        mesh=mesh,
        in_specs=(
            P(None, "blk", None),
            P("blk", "dp"),
            P(None, ("blk", "dp"), None),
            P(("blk", "dp"), None),
            P(("blk", "dp"), None),
            P(("blk", "dp")),
            P(("blk", "dp")),
            P(("blk", "dp")),
            P(("blk", "dp")),
            P(None, ("blk", "dp"), None),
            P(("blk", "dp"), None),
            P(("blk", "dp"), None),
        ),
        out_specs=(P(("blk", "dp"), None), P(("blk", "dp"), None), P("blk", "dp")),
        check_vma=False,
    )
```

profile of v0, /device:TPU:8, one launch (start us, length us, event | category | flops | bytes accessed | tf_op | source)
XLA Modules:
  0.0 180.7 jit_solution(2516782915441205581)
XLA Ops:
  0.6 0.0 copy-start
  0.6 0.0 copy-start.18
  0.7 0.9 convert_element_type.16
  1.5 12.7 %all_to_all.45 = bf16[16,32,128]{2,1,0:T(8,128)(2,1)S(1)} all-to-all(bf16[16,32,128]{2,1,0:T(8,128)(2,1)S(1)} %broadcast_in_dim.16), channel_id=1, replica_groups=mesh['blk'=16,'dp'=32] {'blk'}, dimensions={0} | all-to-all | bytes 262144 | tf_op jit(solution)/shard_map/all_to_all | solution.py:23
  14.2 0.0 copy-done
  14.2 1.2 fusion.50
  15.5 15.3 %all-to-all-start.2 = ((f32[32,32,128]{2,1,0:T(8,128)}), f32[32,32,128]{2,1,0:T(8,128)S(1)}, u32[]{:S(2)}, u32[]{:S(2)}) async-start(f32[32,32,128]{2,1,0:T(8,128)} %fusion.50), calls=%async_computation.2 | async-start | bytes 1048576 | tf_op jit(solution)/shard_map/all_to_all | solution.py:17
  30.7 0.0 copy-done.18
  30.7 0.7 fusion
  31.5 1.1 copy.23
  32.6 0.0 copy-start.7
  32.6 0.0 copy-start.9
  32.6 0.0 copy-start.10
  32.6 0.0 copy-start.12
  32.6 0.0 copy-start.14
  32.6 0.0 copy-start.16
  32.6 18.2 %all-to-all-done.2 = f32[32,32,128]{2,1,0:T(8,128)S(1)} async-done(((f32[32,32,128]{2,1,0:T(8,128)}), f32[32,32,128]{2,1,0:T(8,128)S(1)}, u32[]{:S(2)}, u32[]{:S(2)}) %all-to-all-start.2) | async-done | bytes 524320 | tf_op jit(solution)/shard_map/all_to_all | solution.py:17
  50.9 3.7 %all-to-all-start = ((f32[16,32,4,128]{3,1,2,0:T(8,128)}), f32[16,32,4,128]{3,1,2,0:T(8,128)S(1)}, u32[]{:S(2)}, u32[]{:S(2)}) async-start(f32[16,32,4,128]{3,1,2,0:T(8,128)} %copy.23), calls=%async_computation | async-start | bytes 2097152 | tf_op jit(solution)/shard_map/all_to_all | solution.py:17
  54.5 0.8 dynamic-slice_convert_fusion
  55.4 15.7 %all-to-all-done = f32[16,32,4,128]{3,1,2,0:T(8,128)S(1)} async-done(((f32[16,32,4,128]{3,1,2,0:T(8,128)}), f32[16,32,4,128]{3,1,2,0:T(8,128)S(1)}, u32[]{:S(2)}, u32[]{:S(2)}) %all-to-all-start) | async-done | bytes 1048608 | tf_op jit(solution)/shard_map/all_to_all | solution.py:17
  71.0 0.1 reduce_sum.45
  71.1 0.0 copy-done.3
  71.1 0.0 copy-done.4
  71.1 0.0 copy-done.5
  71.1 0.0 copy-done.6
  71.2 0.0 copy-done.7
  71.2 0.0 copy-done.9
  71.2 0.0 copy-done.10
  71.2 0.0 copy-done.12
  71.2 0.0 copy-done.14
  71.2 0.0 copy-done.16
  71.2 0.1 fusion.46
  71.4 9.3 %all_to_all.46 = bf16[16,32,128]{2,1,0:T(8,128)(2,1)S(1)} all-to-all(bf16[16,32,128]{2,1,0:T(8,128)(2,1)S(1)} %broadcast_in_dim.17), channel_id=1, replica_groups=mesh['blk'=16,'dp'=32] {'blk'}, dimensions={0} | all-to-all | bytes 262144 | tf_op jit(solution)/shard_map/all_to_all | solution.py:23
  80.7 0.5 convolution_bitcast_fusion.3
  81.1 0.2 copy.24
  81.3 25.0 %all_to_all.47 = f32[32,32,128]{2,1,0:T(8,128)S(1)} all-to-all(f32[32,32,128]{2,1,0:T(8,128)S(1)} %bitcast.167), channel_id=1, replica_groups=mesh['blk'=16,'dp'=32] {'dp'}, dimensions={0} | all-to-all | bytes 1048576 | tf_op jit(solution)/shard_map/all_to_all | solution.py:17
  106.3 0.1 fusion.43
  106.5 9.4 %all_to_all.48 = bf16[16,32,128]{2,1,0:T(8,128)(2,1)S(1)} all-to-all(bf16[16,32,128]{2,1,0:T(8,128)(2,1)S(1)} %broadcast_in_dim.18), channel_id=1, replica_groups=mesh['blk'=16,'dp'=32] {'blk'}, dimensions={0} | all-to-all | bytes 262144 | tf_op jit(solution)/shard_map/all_to_all | solution.py:23
  115.9 0.5 convolution_bitcast_fusion.2
  116.3 0.2 copy.25
  116.5 24.8 %all_to_all.49 = f32[32,32,128]{2,1,0:T(8,128)S(1)} all-to-all(f32[32,32,128]{2,1,0:T(8,128)S(1)} %bitcast.168), channel_id=1, replica_groups=mesh['blk'=16,'dp'=32] {'dp'}, dimensions={0} | all-to-all | bytes 1048576 | tf_op jit(solution)/shard_map/all_to_all | solution.py:17
  141.4 0.0 copy-done.1
  141.4 0.1 fusion.41
  141.5 9.4 %all_to_all.50 = bf16[16,32,128]{2,1,0:T(8,128)(2,1)S(1)} all-to-all(bf16[16,32,128]{2,1,0:T(8,128)(2,1)S(1)} %broadcast_in_dim.19), channel_id=1, replica_groups=mesh['blk'=16,'dp'=32] {'blk'}, dimensions={0} | all-to-all | bytes 262144 | tf_op jit(solution)/shard_map/all_to_all | solution.py:23
  150.9 0.5 convolution_bitcast_fusion.1
  151.4 1.0 copy.26
  152.4 4.9 %all-to-all-start.8 = ((f32[32,32,128]{2,1,0:T(8,128)}), f32[32,32,128]{2,1,0:T(8,128)}, u32[]{:S(2)}, u32[]{:S(2)}) async-start(f32[32,32,128]{2,1,0:T(8,128)} %bitcast.27), calls=%async_computation.8 | async-start | bytes 1048576 | tf_op jit(solution)/shard_map/all_to_all | solution.py:17
  157.3 0.0 copy-done.2
  157.4 2.1 %convolution_bitcast_fusion = f32[1024,512]{0,1:T(8,128)S(1)} fusion(bf16[4,1024,128]{2,1,0:T(8,128)(2,1)} %param.12, bf16[1,512,128]{2,1,0:T(8,128)(2,1)S(1)} %bitcast.171, bf16[1,512,128]{2,1,0:T(8,128)(2,1)S(1)} %bitcast.173, bf16[1,512,128]{2,1,0:T(8,128)(2,1)} %bitcast.175, bf16[1,512,128]{2,1,0:T(8,128)(2,1)} %bitcast.177), kind=kOutput, calls=%fused_computation | convolution fusion | flops 537657344 | bytes 3670016 | tf_op jit(solution)/shard_map/tpb,tcb->pc/dot_general | solution.py:102
  159.5 0.0 copy-start.8
  159.5 0.0 copy-start.11
  159.5 0.0 copy-start.13
  159.5 0.0 copy-start.15
  159.5 0.0 copy-start.17
  159.5 1.8 %copy.27 = f32[1024,512]{1,0:T(8,128)} copy(f32[1024,512]{0,1:T(8,128)S(1)} %convolution_bitcast_fusion) | data formatting | bytes 4194304
  161.4 16.2 %all-to-all-done.8 = f32[32,32,128]{2,1,0:T(8,128)} async-done(((f32[32,32,128]{2,1,0:T(8,128)}), f32[32,32,128]{2,1,0:T(8,128)}, u32[]{:S(2)}, u32[]{:S(2)}) %all-to-all-start.8) | async-done | bytes 524320 | tf_op jit(solution)/shard_map/all_to_all | solution.py:17
  177.5 1.1 reduce_sum.49
  178.6 0.0 copy-done.8
  178.6 0.0 copy-done.11
  178.6 0.0 copy-done.13
  178.6 0.0 copy-done.15
  178.6 1.4 multiply_subtract_fusion
  180.1 0.0 copy-done.17
  180.1 0.7 multiply_add_fusion
  (13 shorter events, 0.2 us)
Async XLA Ops:
  0.6 13.6 %copy-start = (bf16[1024,512]{1,0:T(8,128)(2,1)S(1)}, bf16[1024,512]{1,0:T(8,128)(2,1)}, u32[]{:S(2)}) copy-start(bf16[1024,512]{1,0:T(8,128)(2,1)} %param.13) | copy-start | bytes 3145732
  0.6 30.1 %copy-start.18 = (bf16[4,1024,128]{2,1,0:T(8,128)(2,1)S(1)}, bf16[4,1024,128]{2,1,0:T(8,128)(2,1)}, u32[]{:S(2)}) copy-start(bf16[4,1024,128]{2,1,0:T(8,128)(2,1)} %param.12) | copy-start | bytes 3145732
  15.5 35.4 %all-to-all-start.2 = ((f32[32,32,128]{2,1,0:T(8,128)}), f32[32,32,128]{2,1,0:T(8,128)S(1)}, u32[]{:S(2)}, u32[]{:S(2)}) async-start(f32[32,32,128]{2,1,0:T(8,128)} %fusion.50), calls=%async_computation.2 | async-start | bytes 1048576 | tf_op jit(solution)/shard_map/all_to_all | solution.py:17
  32.5 38.6 %copy-start.3 = (f32[32,128]{1,0:T(8,128)S(1)}, f32[32,128]{1,0:T(8,128)}, u32[]{:S(2)}) copy-start(f32[32,128]{1,0:T(8,128)} %param.22) | copy-start | bytes 49156
  32.5 38.6 %copy-start.4 = (f32[4,32,128]{2,1,0:T(8,128)S(1)}, f32[4,32,128]{2,1,0:T(8,128)}, u32[]{:S(2)}) copy-start(f32[4,32,128]{2,1,0:T(8,128)} %param.21) | copy-start | bytes 196612
  32.5 38.6 %copy-start.5 = (f32[32,128]{1,0:T(8,128)S(1)}, f32[32,128]{1,0:T(8,128)}, u32[]{:S(2)}) copy-start(f32[32,128]{1,0:T(8,128)} %param.23) | copy-start | bytes 49156
  32.5 38.6 %copy-start.6 = (f32[32,128]{1,0:T(8,128)S(1)}, f32[32,128]{1,0:T(8,128)}, u32[]{:S(2)}) copy-start(f32[32,128]{1,0:T(8,128)} %param.16) | copy-start | bytes 49156
  32.6 38.6 %copy-start.7 = (f32[32,128]{1,0:T(8,128)S(1)}, f32[32,128]{1,0:T(8,128)}, u32[]{:S(2)}) copy-start(f32[32,128]{1,0:T(8,128)} %param.15) | copy-start | bytes 49156
  32.6 38.6 %copy-start.9 = (f32[4,32,128]{2,1,0:T(8,128)S(1)}, f32[4,32,128]{2,1,0:T(8,128)}, u32[]{:S(2)}) copy-start(f32[4,32,128]{2,1,0:T(8,128)} %param.14) | copy-start | bytes 196612
  32.6 38.6 %copy-start.10 = (f32[32]{0:T(128)S(1)}, f32[32]{0:T(128)}, u32[]{:S(2)}) copy-start(f32[32]{0:T(128)} %param.18) | copy-start | bytes 388
  32.6 38.6 %copy-start.12 = (f32[32]{0:T(128)S(1)}, f32[32]{0:T(128)}, u32[]{:S(2)}) copy-start(f32[32]{0:T(128)} %param.19) | copy-start | bytes 388
  32.6 38.6 %copy-start.14 = (f32[32]{0:T(128)S(1)}, f32[32]{0:T(128)}, u32[]{:S(2)}) copy-start(f32[32]{0:T(128)} %param.20) | copy-start | bytes 388
  32.6 38.6 %copy-start.16 = (f32[32]{0:T(128)S(1)}, f32[32]{0:T(128)}, u32[]{:S(2)}) copy-start(f32[32]{0:T(128)} %param.17) | copy-start | bytes 388
  50.9 20.2 %all-to-all-start = ((f32[16,32,4,128]{3,1,2,0:T(8,128)}), f32[16,32,4,128]{3,1,2,0:T(8,128)S(1)}, u32[]{:S(2)}, u32[]{:S(2)}) async-start(f32[16,32,4,128]{3,1,2,0:T(8,128)} %copy.23), calls=%async_computation | async-start | bytes 2097152 | tf_op jit(solution)/shard_map/all_to_all | solution.py:17
  115.9 25.5 %copy-start.1 = (bf16[16,32,128]{2,1,0:T(8,128)(2,1)}, bf16[16,32,128]{2,1,0:T(8,128)(2,1)S(1)}, u32[]{:S(2)}) copy-start(bf16[16,32,128]{2,1,0:T(8,128)(2,1)S(1)} %all_to_all.48) | copy-start | bytes 393220
  150.9 6.4 %copy-start.2 = (bf16[16,32,128]{2,1,0:T(8,128)(2,1)}, bf16[16,32,128]{2,1,0:T(8,128)(2,1)S(1)}, u32[]{:S(2)}) copy-start(bf16[16,32,128]{2,1,0:T(8,128)(2,1)S(1)} %all_to_all.50) | copy-start | bytes 393220
  152.4 25.1 %all-to-all-start.8 = ((f32[32,32,128]{2,1,0:T(8,128)}), f32[32,32,128]{2,1,0:T(8,128)}, u32[]{:S(2)}, u32[]{:S(2)}) async-start(f32[32,32,128]{2,1,0:T(8,128)} %bitcast.27), calls=%async_computation.8 | async-start | bytes 1048576 | tf_op jit(solution)/shard_map/all_to_all | solution.py:17
  159.5 19.1 %copy-start.8 = (f32[32,128]{1,0:T(8,128)S(1)}, f32[32,128]{1,0:T(8,128)}, u32[]{:S(2)}) copy-start(f32[32,128]{1,0:T(8,128)} %param.15) | copy-start | bytes 49156
  159.5 19.1 %copy-start.11 = (f32[32]{0:T(128)S(1)}, f32[32]{0:T(128)}, u32[]{:S(2)}) copy-start(f32[32]{0:T(128)} %param.18) | copy-start | bytes 388
  159.5 19.1 %copy-start.13 = (f32[32]{0:T(128)S(1)}, f32[32]{0:T(128)}, u32[]{:S(2)}) copy-start(f32[32]{0:T(128)} %param.19) | copy-start | bytes 388
  159.5 19.1 %copy-start.15 = (f32[32]{0:T(128)S(1)}, f32[32]{0:T(128)}, u32[]{:S(2)}) copy-start(f32[32]{0:T(128)} %param.20) | copy-start | bytes 388
  159.5 20.5 %copy-start.17 = (f32[32]{0:T(128)S(1)}, f32[32]{0:T(128)}, u32[]{:S(2)}) copy-start(f32[32]{0:T(128)} %param.17) | copy-start | bytes 388
where the time goes:
time: 182 us; the launch traced here: 181 us
  blocking collectives  90.5 us (50%)
  waiting for transfers between devices  50.1 us (28%)
  starting transfers between devices  23.9 us (13%)
  matrix products  5.49 us (3%)
  other arithmetic  5.34 us (3%)
  local copies, waits for them, and re-layouts  4.45 us (2%)
    all_to_all x3, waiting for transfers between devices, summed_on_arrival(): lax.all_to_all(cut_along(shard, dim, length), axis, 0, 0, tiled=True)  50.1 us
    all_to_all x2, blocking collectives, summed_on_arrival(): lax.all_to_all(cut_along(shard, dim, length), axis, 0, 0, tiled=True)  49.8 us
    all_to_all x4, blocking collectives, copy_for_each(): return lax.all_to_all(copies, axis, split_axis=0, concat_axis=0, tiled=True)  40.8 us
    all_to_all x3, starting transfers between devices, summed_on_arrival(): lax.all_to_all(cut_along(shard, dim, length), axis, 0, 0, tiled=True)  23.9 us
  transfers between devices with their start and end apart: 3, of which 3 were waited for; matrix products, arithmetic and copies ran while one was open for 4% of the time, Pallas kernels for 0%

commit v1 on v0

v1 whole, which is shorter than its diff:
```python
import jax
import jax.numpy as jnp
from jax import lax
from jax.sharding import PartitionSpec as P

pseudo_derivative_factor = 0.5
bf16 = jnp.bfloat16
f32 = jnp.float32


def exchange(parts, axis):
    return lax.all_to_all(parts, axis, 0, 0, tiled=True)


def row_partials(weights, pieces, num_dp):
    part = jnp.dot(weights, pieces, preferred_element_type=f32).astype(bf16)
    return part.reshape(num_dp, -1, part.shape[-1])


def body(
    spikes,
    rec_weights,
    in_current,
    volt_init,
    adapt_init,
    mem_decay,
    adapt_decay,
    adapt_gain,
    resting_trigger_level,
    pulse_sensitivity,
    volt_cot,
    adapt_cot,
):
    num_steps = spikes.shape[0]
    own, trials = volt_init.shape
    num_blk = lax.axis_size("blk")
    num_dp = lax.axis_size("dp")
    own_fired = lax.dynamic_slice_in_dim(
        spikes, lax.axis_index("dp") * own, own, 1
    ).astype(f32)
    leak_rate = mem_decay[:, None]
    keep_rate = adapt_decay[:, None]
    gain_col = adapt_gain[:, None]
    minimum_column = resting_trigger_level[:, None]

    outgoing = [
        lax.dot_general(
            rec_weights, spikes[t], (((0,), (0,)), ((), ())), preferred_element_type=f32
        )
        .astype(bf16)
        .reshape(num_blk, 1, own, trials)
        for t in range(num_steps - 1)
    ]
    outgoing.append(
        jnp.broadcast_to(volt_cot.astype(bf16), (num_blk, 1, own, trials))
    )
    arrived = exchange(jnp.concatenate(outgoing, axis=1), "blk")
    currents = jnp.sum(arrived[:, : num_steps - 1].astype(f32), axis=0)
    pieces = arrived[:, num_steps - 1].reshape(num_blk * own, trials)

    voltage = volt_init
    adaptation = adapt_init
    threshold_values = []
    surrogates = []
    for t in range(num_steps):
        thresh = minimum_column + gain_col * adaptation
        surrogates.append(
            pseudo_derivative_factor / jnp.square(1.0 + jnp.abs(voltage - thresh))
        )
        threshold_values.append(thresh)
        if t + 1 < num_steps:
            voltage = (
                leak_rate * voltage + currents[t] + in_current[t] - thresh * own_fired[t]
            )
            adaptation = keep_rate * adaptation + own_fired[t]

    volt_adj = volt_cot
    adapt_adj = adapt_cot
    kept_pieces = []
    for t in reversed(range(num_steps)):
        kept_pieces.insert(0, pieces)
        partials = exchange(row_partials(rec_weights, pieces, num_dp), "dp")
        recurrent = jnp.sum(partials.astype(f32), axis=0)
        spike_adj = (
            pulse_sensitivity[t]
            + recurrent
            - threshold_values[t] * volt_adj
            + adapt_adj
        )
        through = surrogates[t] * spike_adj
        new_volt = leak_rate * volt_adj + through
        adapt_adj = keep_rate * adapt_adj - gain_col * (own_fired[t] * volt_adj + through)
        volt_adj = new_volt
        if t > 0:
            copies = jnp.broadcast_to(volt_adj.astype(bf16), (num_blk, own, trials))
            pieces = exchange(copies, "blk").reshape(num_blk * own, trials)
    weight_sum = jnp.einsum(
        "tpb,tcb->pc", spikes, jnp.stack(kept_pieces), preferred_element_type=f32
    )
    return (volt_adj, adapt_adj, weight_sum)


def solution(mesh):
    own = P(("blk", "dp"))
    window = P(None, ("blk", "dp"))
    return jax.shard_map(
        body,
        mesh=mesh,
        in_specs=(
            P(None, "blk"),
            P("blk", "dp"),
            window,
            own,
            own,
            own,
            own,
            own,
            own,
            window,
            own,
            own,
        ),
        out_specs=(own, own, P("blk", "dp")),
        check_vma=False,
    )
```

time: 182 us -> 146 us (0.80)
  the two profiles are of different devices: /device:TPU:8 before, /device:TPU:1 now
where the time goes in v1:
time: 146 us; the launch traced here: 143 us
  blocking collectives  87.5 us (60%)
  waiting for transfers between devices  20 us (14%)
  starting transfers between devices  16.7 us (11%)
  matrix products  8.47 us (6%)
  local copies, waits for them, and re-layouts  5.2 us (4%)
  other arithmetic  4.2 us (3%)
    all_to_all x6, blocking collectives, exchange(): return lax.all_to_all(parts, axis, 0, 0, tiled=True)  87.5 us
    all_to_all x2, waiting for transfers between devices, exchange(): return lax.all_to_all(parts, axis, 0, 0, tiled=True)  20 us
    all_to_all x2, starting transfers between devices, exchange(): return lax.all_to_all(parts, axis, 0, 0, tiled=True)  16.7 us
    dot_general x3, matrix products, body(): lax.dot_general(rec_weights, spikes[t], (((0,), (0,)), ((), ())), preferr...  4.31 us
    unnamed x31, local copies, waits for them, and re-layouts  3.1 us
  transfers between devices with their start and end apart: 2, of which 2 were waited for; matrix products, arithmetic and copies ran while one was open for 3% of the time, Pallas kernels for 0%

profile of v1, /device:TPU:1, one launch (start us, length us, event | category | flops | bytes accessed | tf_op | source)
XLA Modules:
  0.0 143.0 jit_solution(11375922629912492886)
XLA Ops:
  0.6 0.0 copy-start
  0.6 0.0 copy-start.5
  0.7 1.2 copy-done
  1.9 1.4 %convolution_convert_fusion.4 = bf16[512,128]{1,0:T(8,128)(2,1)S(1)} fusion(bf16[1024,512]{1,0:T(8,128)(2,1)S(1)} %copy-done, bf16[4,1024,128]{2,1,0:T(8,128)(2,1)} %param.12), kind=kOutput, calls=%fused_computation.9 | convolution fusion | flops 134283264 | bytes 1441792 | tf_op jit(solution)/shard_map/dot_general | solution.py:47
  3.3 1.4 %convolution_convert_fusion.5 = bf16[512,128]{1,0:T(8,128)(2,1)S(1)} fusion(bf16[1024,512]{1,0:T(8,128)(2,1)S(1)} %copy-done, bf16[4,1024,128]{2,1,0:T(8,128)(2,1)} %param.12), kind=kOutput, calls=%fused_computation.10 | convolution fusion | flops 134283264 | bytes 1441792 | tf_op jit(solution)/shard_map/dot_general | solution.py:47
  4.7 1.4 %convolution_convert_fusion.6 = bf16[512,128]{1,0:T(8,128)(2,1)S(1)} fusion(bf16[1024,512]{1,0:T(8,128)(2,1)S(1)} %copy-done, bf16[4,1024,128]{2,1,0:T(8,128)(2,1)} %param.12), kind=kOutput, calls=%fused_computation.11 | convolution fusion | flops 134283264 | bytes 1441792 | tf_op jit(solution)/shard_map/dot_general | solution.py:47
  6.2 0.0 copy-done.5
  6.2 0.1 pad_maximum_fusion
  6.3 0.0 copy-start.6
  6.3 0.0 copy-start.7
  6.3 0.0 copy-start.8
  6.3 0.0 copy-start.9
  6.4 0.0 copy-start.10
  6.4 0.0 copy-start.11
  6.4 0.0 copy-start.12
  6.4 0.0 copy-start.13
  6.4 0.0 copy-start.14
  6.4 19.2 %all_to_all.40 = bf16[16,4,32,128]{3,2,1,0:T(8,128)(2,1)S(1)} all-to-all(bf16[16,4,32,128]{3,2,1,0:T(8,128)(2,1)S(1)} %pad_maximum_fusion), channel_id=1, replica_groups=mesh['blk'=16,'dp'=32] {'blk'}, dimensions={0} | all-to-all | bytes 1048576 | tf_op jit(solution)/shard_map/all_to_all | solution.py:12
  25.6 0.0 copy-start.1
  25.6 0.5 fusion
  26.1 0.8 copy.24
  26.9 12.8 %all-to-all-start.1 = ((bf16[32,32,128]{2,1,0:T(8,128)(2,1)}), bf16[32,32,128]{2,1,0:T(8,128)(2,1)S(1)}, u32[]{:S(2)}, u32[]{:S(2)}) async-start(bf16[32,32,128]{2,1,0:T(8,128)(2,1)} %bitcast.21), calls=%async_computation.1 | async-start | bytes 524288 | tf_op jit(solution)/shard_map/all_to_all | solution.py:12
  39.8 0.8 dynamic-slice_convert_fusion
  40.5 0.1 convert_reduce_fusion
  40.6 11.6 %all-to-all-done.1 = bf16[32,32,128]{2,1,0:T(8,128)(2,1)S(1)} async-done(((bf16[32,32,128]{2,1,0:T(8,128)(2,1)}), bf16[32,32,128]{2,1,0:T(8,128)(2,1)S(1)}, u32[]{:S(2)}, u32[]{:S(2)}) %all-to-all-start.1) | async-done | bytes 262176 | tf_op jit(solution)/shard_map/all_to_all | solution.py:12
  52.3 0.0 copy-done.6
  52.3 0.0 copy-done.7
  52.3 0.0 copy-done.8
  52.3 0.0 copy-done.9
  52.3 0.0 copy-done.10
  52.3 0.0 copy-done.11
  52.3 0.0 copy-done.12
  52.3 0.0 copy-done.13
  52.4 0.0 copy-done.14
  52.4 0.1 fusion.54
  52.5 12.2 %all_to_all.41 = bf16[16,32,128]{2,1,0:T(8,128)(2,1)S(1)} all-to-all(bf16[16,32,128]{2,1,0:T(8,128)(2,1)S(1)} %broadcast_in_dim.17), channel_id=1, replica_groups=mesh['blk'=16,'dp'=32] {'blk'}, dimensions={0} | all-to-all | bytes 262144 | tf_op jit(solution)/shard_map/all_to_all | solution.py:12
  64.7 0.0 copy-start.2
  64.7 0.5 fusion.1
  65.2 0.0 copy-done.1
  65.2 0.2 copy.25
  65.4 16.1 %all_to_all.42 = bf16[32,32,128]{2,1,0:T(8,128)(2,1)S(1)} all-to-all(bf16[32,32,128]{2,1,0:T(8,128)(2,1)S(1)} %bitcast.182), channel_id=1, replica_groups=mesh['blk'=16,'dp'=32] {'dp'}, dimensions={0} | all-to-all | bytes 524288 | tf_op jit(solution)/shard_map/all_to_all | solution.py:12
  81.6 0.1 fusion.51
  81.7 12.0 %all_to_all.43 = bf16[16,32,128]{2,1,0:T(8,128)(2,1)S(1)} all-to-all(bf16[16,32,128]{2,1,0:T(8,128)(2,1)S(1)} %broadcast_in_dim.18), channel_id=1, replica_groups=mesh['blk'=16,'dp'=32] {'blk'}, dimensions={0} | all-to-all | bytes 262144 | tf_op jit(solution)/shard_map/all_to_all | solution.py:12
  93.8 0.0 copy-start.3
  93.8 0.5 fusion.2
  94.3 0.0 copy-done.2
  94.3 0.2 copy.26
  94.4 15.8 %all_to_all.44 = bf16[32,32,128]{2,1,0:T(8,128)(2,1)S(1)} all-to-all(bf16[32,32,128]{2,1,0:T(8,128)(2,1)S(1)} %bitcast.183), channel_id=1, replica_groups=mesh['blk'=16,'dp'=32] {'dp'}, dimensions={0} | all-to-all | bytes 524288 | tf_op jit(solution)/shard_map/all_to_all | solution.py:12
  110.3 0.1 fusion.49
  110.5 12.0 %all_to_all.45 = bf16[16,32,128]{2,1,0:T(8,128)(2,1)S(1)} all-to-all(bf16[16,32,128]{2,1,0:T(8,128)(2,1)S(1)} %broadcast_in_dim.19), channel_id=1, replica_groups=mesh['blk'=16,'dp'=32] {'blk'}, dimensions={0} | all-to-all | bytes 262144 | tf_op jit(solution)/shard_map/all_to_all | solution.py:12
  122.5 0.0 copy-start.4
  122.5 0.5 fusion.3
  123.0 0.0 copy-done.3
  123.0 0.8 copy.27
  123.8 3.9 %all-to-all-start.7 = ((bf16[32,32,128]{2,1,0:T(8,128)(2,1)}), bf16[32,32,128]{2,1,0:T(8,128)(2,1)S(1)}, u32[]{:S(2)}, u32[]{:S(2)}) async-start(bf16[32,32,128]{2,1,0:T(8,128)(2,1)} %bitcast.34), calls=%async_computation.7 | async-start | bytes 524288 | tf_op jit(solution)/shard_map/all_to_all | solution.py:12
  127.7 0.0 copy-done.4
  127.7 2.2 %convolution_bitcast_fusion = f32[1024,512]{0,1:T(8,128)S(1)} fusion(bf16[4,1024,128]{2,1,0:T(8,128)(2,1)} %param.12, bf16[1,512,128]{2,1,0:T(8,128)(2,1)} %bitcast.185, bf16[1,512,128]{2,1,0:T(8,128)(2,1)} %bitcast.187, bf16[1,512,128]{2,1,0:T(8,128)(2,1)} %bitcast.189, bf16[1,512,128]{2,1,0:T(8,128)(2,1)} %bitcast.191), kind=kOutput, calls=%fused_computation | convolution fusion | flops 537657344 | bytes 3670016 | tf_op jit(solution)/shard_map/tpb,tcb->pc/dot_general | solution.py:97
  130.0 1.8 %copy.28 = f32[1024,512]{1,0:T(8,128)} copy(f32[1024,512]{0,1:T(8,128)S(1)} %convolution_bitcast_fusion) | data formatting | bytes 4194304
  131.8 8.4 %all-to-all-done.7 = bf16[32,32,128]{2,1,0:T(8,128)(2,1)S(1)} async-done(((bf16[32,32,128]{2,1,0:T(8,128)(2,1)}), bf16[32,32,128]{2,1,0:T(8,128)(2,1)S(1)}, u32[]{:S(2)}, u32[]{:S(2)}) %all-to-all-start.7) | async-done | bytes 262176 | tf_op jit(solution)/shard_map/all_to_all | solution.py:12
  140.2 1.5 %multiply_subtract_fusion = (f32[32,128]{1,0:T(8,128)}, f32[32,128]{1,0:T(8,128)S(1)}) fusion(f32[32,128]{1,0:T(8,128)S(1)} %get-tuple-element.15, f32[4,32,128]{2,1,0:T(8,128)S(1)} %dynamic-slice_convert_fusion, f32[32]{0:T(128)} %param.18, f32[32]{0:T(128)} %param.19, f32[32,128]{1,0:T(8,128)S(1)} %convert_reduce_fusion.1, f32[4,32,128]{2,1,0:T(8,128)} %param.21, ...), kind=kLoop, calls=%fused_computation.73 | loop fusion | flops 90112 | bytes 196992 | tf_op jit(solution)/shard_map/sub | solution.py:92
  141.7 1.3 multiply_add_fusion
  (10 shorter events, 0.3 us)
Async XLA Ops:
  0.6 1.2 copy-start
  0.6 5.5 %copy-start.5 = (f32[32,128]{1,0:T(8,128)S(1)}, f32[32,128]{1,0:T(8,128)}, u32[]{:S(2)}) copy-start(f32[32,128]{1,0:T(8,128)} %param.22) | copy-start | bytes 49156
  6.3 46.0 %copy-start.6 = (f32[4,32,128]{2,1,0:T(8,128)S(1)}, f32[4,32,128]{2,1,0:T(8,128)}, u32[]{:S(2)}) copy-start(f32[4,32,128]{2,1,0:T(8,128)} %param.21) | copy-start | bytes 196612
  6.3 46.0 %copy-start.7 = (f32[32,128]{1,0:T(8,128)S(1)}, f32[32,128]{1,0:T(8,128)}, u32[]{:S(2)}) copy-start(f32[32,128]{1,0:T(8,128)} %param.23) | copy-start | bytes 49156
  6.3 46.0 %copy-start.8 = (f32[32,128]{1,0:T(8,128)S(1)}, f32[32,128]{1,0:T(8,128)}, u32[]{:S(2)}) copy-start(f32[32,128]{1,0:T(8,128)} %param.16) | copy-start | bytes 49156
  6.3 46.0 %copy-start.9 = (f32[32,128]{1,0:T(8,128)S(1)}, f32[32,128]{1,0:T(8,128)}, u32[]{:S(2)}) copy-start(f32[32,128]{1,0:T(8,128)} %param.15) | copy-start | bytes 49156
  6.4 46.0 %copy-start.10 = (f32[4,32,128]{2,1,0:T(8,128)S(1)}, f32[4,32,128]{2,1,0:T(8,128)}, u32[]{:S(2)}) copy-start(f32[4,32,128]{2,1,0:T(8,128)} %param.14) | copy-start | bytes 196612
  6.4 46.0 %copy-start.11 = (f32[32]{0:T(128)S(1)}, f32[32]{0:T(128)}, u32[]{:S(2)}) copy-start(f32[32]{0:T(128)} %param.18) | copy-start | bytes 388
  6.4 46.0 %copy-start.12 = (f32[32]{0:T(128)S(1)}, f32[32]{0:T(128)}, u32[]{:S(2)}) copy-start(f32[32]{0:T(128)} %param.19) | copy-start | bytes 388
  6.4 46.0 %copy-start.13 = (f32[32]{0:T(128)S(1)}, f32[32]{0:T(128)}, u32[]{:S(2)}) copy-start(f32[32]{0:T(128)} %param.20) | copy-start | bytes 388
  6.4 46.0 %copy-start.14 = (f32[32]{0:T(128)S(1)}, f32[32]{0:T(128)}, u32[]{:S(2)}) copy-start(f32[32]{0:T(128)} %param.17) | copy-start | bytes 388
  25.6 39.6 %copy-start.1 = (bf16[16,1,32,128]{3,2,1,0:T(8,128)(2,1)}, bf16[16,1,32,128]{3,2,1,0:T(8,128)(2,1)S(1)}, u32[]{:S(2)}) copy-start(bf16[16,1,32,128]{3,2,1,0:T(8,128)(2,1)S(1)} %slice.89) | copy-start | bytes 393220
  26.9 25.3 %all-to-all-start.1 = ((bf16[32,32,128]{2,1,0:T(8,128)(2,1)}), bf16[32,32,128]{2,1,0:T(8,128)(2,1)S(1)}, u32[]{:S(2)}, u32[]{:S(2)}) async-start(bf16[32,32,128]{2,1,0:T(8,128)(2,1)} %bitcast.21), calls=%async_computation.1 | async-start | bytes 524288 | tf_op jit(solution)/shard_map/all_to_all | solution.py:12
  64.7 29.5 %copy-start.2 = (bf16[16,32,128]{2,1,0:T(8,128)(2,1)}, bf16[16,32,128]{2,1,0:T(8,128)(2,1)S(1)}, u32[]{:S(2)}) copy-start(bf16[16,32,128]{2,1,0:T(8,128)(2,1)S(1)} %all_to_all.41) | copy-start | bytes 393220
  93.8 29.2 %copy-start.3 = (bf16[16,32,128]{2,1,0:T(8,128)(2,1)}, bf16[16,32,128]{2,1,0:T(8,128)(2,1)S(1)}, u32[]{:S(2)}) copy-start(bf16[16,32,128]{2,1,0:T(8,128)(2,1)S(1)} %all_to_all.43) | copy-start | bytes 393220
  122.5 5.2 %copy-start.4 = (bf16[16,32,128]{2,1,0:T(8,128)(2,1)}, bf16[16,32,128]{2,1,0:T(8,128)(2,1)S(1)}, u32[]{:S(2)}) copy-start(bf16[16,32,128]{2,1,0:T(8,128)(2,1)S(1)} %all_to_all.45) | copy-start | bytes 393220
  123.8 16.3 %all-to-all-start.7 = ((bf16[32,32,128]{2,1,0:T(8,128)(2,1)}), bf16[32,32,128]{2,1,0:T(8,128)(2,1)S(1)}, u32[]{:S(2)}, u32[]{:S(2)}) async-start(bf16[32,32,128]{2,1,0:T(8,128)(2,1)} %bitcast.34), calls=%async_computation.7 | async-start | bytes 524288 | tf_op jit(solution)/shard_map/all_to_all | solution.py:12

commit v2 on v1

--- a/solution.py
+++ b/solution.py
@@ -15,6 +15,16 @@
 def row_partials(weights, pieces, num_dp):
     part = jnp.dot(weights, pieces, preferred_element_type=f32).astype(bf16)
     return part.reshape(num_dp, -1, part.shape[-1])
+
+
+def halve(total, bit):
+    size = lax.axis_size("blk")
+    mine = (lax.axis_index("blk") // bit) % 2
+    pairs = total.reshape(total.shape[0] // 2, 2, *total.shape[1:])
+    sent = jnp.where(mine == 0, pairs[:, 1], pairs[:, 0]).astype(bf16)
+    got = lax.ppermute(sent, "blk", [(s, s ^ bit) for s in range(size)])
+    kept = jnp.where(mine == 0, pairs[:, 0], pairs[:, 1])
+    return kept + got.astype(f32)
 
 
 def body(
@@ -43,20 +53,23 @@
     gain_col = adapt_gain[:, None]
     minimum_column = resting_trigger_level[:, None]
 
-    outgoing = [
-        lax.dot_general(
-            rec_weights, spikes[t], (((0,), (0,)), ((), ())), preferred_element_type=f32
-        )
-        .astype(bf16)
-        .reshape(num_blk, 1, own, trials)
-        for t in range(num_steps - 1)
-    ]
-    outgoing.append(
-        jnp.broadcast_to(volt_cot.astype(bf16), (num_blk, 1, own, trials))
-    )
-    arrived = exchange(jnp.concatenate(outgoing, axis=1), "blk")
-    currents = jnp.sum(arrived[:, : num_steps - 1].astype(f32), axis=0)
-    pieces = arrived[:, num_steps - 1].reshape(num_blk * own, trials)
+    def gathered(values):
+        copies = jnp.broadcast_to(values.astype(bf16), (num_blk, own, trials))
+        return exchange(copies, "blk").reshape(num_blk * own, trials)
+
+    pieces = gathered(volt_cot)
+    total = jnp.einsum(
+        "pc,tpb->ctb",
+        rec_weights,
+        spikes[: num_steps - 1],
+        preferred_element_type=f32,
+    ).reshape(num_blk, own, num_steps - 1, trials)
+    bit = 1
+    while bit < num_blk:
+        total = halve(total, bit)
+        bit *= 2
+    currents = total[0]
+    partials = exchange(row_partials(rec_weights, pieces, num_dp), "dp")
 
     voltage = volt_init
     adaptation = adapt_init
@@ -70,7 +83,10 @@
         threshold_values.append(thresh)
         if t + 1 < num_steps:
             voltage = (
-                leak_rate * voltage + currents[t] + in_current[t] - thresh * own_fired[t]
+                leak_rate * voltage
+                + currents[:, t]
+                + in_current[t]
+                - thresh * own_fired[t]
             )
             adaptation = keep_rate * adaptation + own_fired[t]
 
@@ -79,21 +95,18 @@
     kept_pieces = []
     for t in reversed(range(num_steps)):
         kept_pieces.insert(0, pieces)
-        partials = exchange(row_partials(rec_weights, pieces, num_dp), "dp")
+        if t + 1 < num_steps:
+            partials = exchange(row_partials(rec_weights, pieces, num_dp), "dp")
+        known = pulse_sensitivity[t] - threshold_values[t] * volt_adj + adapt_adj
+        volt_known = leak_rate * volt_adj + surrogates[t] * known
+        adapt_known = keep_rate * adapt_adj - gain_col * (
+            own_fired[t] * volt_adj + surrogates[t] * known
+        )
         recurrent = jnp.sum(partials.astype(f32), axis=0)
-        spike_adj = (
-            pulse_sensitivity[t]
-            + recurrent
-            - threshold_values[t] * volt_adj
-            + adapt_adj
-        )
-        through = surrogates[t] * spike_adj
-        new_volt = leak_rate * volt_adj + through
-        adapt_adj = keep_rate * adapt_adj - gain_col * (own_fired[t] * volt_adj + through)
-        volt_adj = new_volt
+        volt_adj = volt_known + surrogates[t] * recurrent
+        adapt_adj = adapt_known - gain_col * surrogates[t] * recurrent
         if t > 0:
-            copies = jnp.broadcast_to(volt_adj.astype(bf16), (num_blk, own, trials))
-            pieces = exchange(copies, "blk").reshape(num_blk * own, trials)
+            pieces = gathered(volt_adj)
     weight_sum = jnp.einsum(
         "tpb,tcb->pc", spikes, jnp.stack(kept_pieces), preferred_element_type=f32
     )

time: 146 us -> 148 us (1.014)
  starting transfers between devices: 16.7 us -> 37.2 us
  blocking collectives: 87.5 us -> 68.5 us
  matrix products: 8.47 us -> 6.66 us
    all_to_all x6 -> x5, blocking collectives: 87.5 us -> 68.5 us  [exchange(): return lax.all_to_all(parts, axis, 0, 0, tiled=True)]
    ppermute x0 -> x4, starting transfers between devices: none -> 16.8 us  [halve(): got = lax.ppermute(sent, 'blk', [(s, s ^ bit) for s in range(size)])]
    all_to_all x2 -> x3, starting transfers between devices: 16.7 us -> 20.4 us  [exchange(): return lax.all_to_all(parts, axis, 0, 0, tiled=True)]
    ppermute x0 -> x4, waiting for transfers between devices: none -> 3.66 us  [halve(): got = lax.ppermute(sent, 'blk', [(s, s ^ bit) for s in range(size)])]
    all_to_all x2 -> x3, waiting for transfers between devices: 20 us -> 17.3 us  [exchange(): return lax.all_to_all(parts, axis, 0, 0, tiled=True)]
    dot_general x3 -> x1, matrix products: 4.31 us -> 1.87 us  [body(): jnp.einsum('pc,tpb->ctb', rec_weights, spikes[:num_steps - 1], preferred_...]
    unnamed x31 -> x39, local copies, waits for them, and re-layouts: 3.1 us -> 3.11 us
  transfers between devices with their start and end apart: 2 -> 7, of which waited for: 2 -> 5; matrix products, arithmetic and copies ran while one was open for 3% -> 5% of each run, Pallas kernels for 0% -> 0%
where the time goes in v2:
time: 148 us; the launch traced here: 145 us
  blocking collectives  68.5 us (46%)
  starting transfers between devices  37.2 us (25%)
  waiting for transfers between devices  20.9 us (14%)
  matrix products  6.66 us (4%)
  other arithmetic  5.16 us (3%)
  local copies, waits for them, and re-layouts  5.07 us (3%)
    all_to_all x5, blocking collectives, exchange(): return lax.all_to_all(parts, axis, 0, 0, tiled=True)  68.5 us
    all_to_all x3, starting transfers between devices, exchange(): return lax.all_to_all(parts, axis, 0, 0, tiled=True)  20.4 us
    all_to_all x3, waiting for transfers between devices, exchange(): return lax.all_to_all(parts, axis, 0, 0, tiled=True)  17.3 us
    ppermute x4, starting transfers between devices, halve(): got = lax.ppermute(sent, 'blk', [(s, s ^ bit) for s in range(size)])  16.8 us
    ppermute x4, waiting for transfers between devices, halve(): got = lax.ppermute(sent, 'blk', [(s, s ^ bit) for s in range(size)])  3.66 us
    unnamed x39, local copies, waits for them, and re-layouts  3.11 us
  transfers between devices with their start and end apart: 7, of which 5 were waited for; matrix products, arithmetic and copies ran while one was open for 5% of the time, Pallas kernels for 0%

profile of v2, /device:TPU:1, one launch (start us, length us, event | category | flops | bytes accessed | tf_op | source)
XLA Modules:
  0.0 144.6 jit_solution(2765767411927261247)
XLA Ops:
  0.6 0.0 copy-start
  0.7 1.2 copy-done
  1.9 1.9 %fusion.3 = f32[512,3,128]{2,0,1:T(8,128)S(1)} fusion(bf16[1024,512]{1,0:T(8,128)(2,1)S(1)} %copy-done, bf16[4,1024,128]{2,1,0:T(8,128)(2,1)} %param.12), kind=kOutput, calls=%fused_computation.8 | convolution fusion | flops 402653184 | bytes 2621440 | tf_op jit(solution)/shard_map/pc,tpb->ctb/dot_general | solution.py:61
  3.7 0.0 copy-start.6
  3.7 0.1 fusion.57
  3.9 8.8 %collective-permute-start = (bf16[8,32,3,128]{3,1,2,0:T(8,128)(2,1)S(1)}, bf16[8,32,3,128]{3,1,2,0:T(8,128)(2,1)S(1)}, u32[]{:S(2)}, u32[]{:S(2)}) collective-permute-start(bf16[8,32,3,128]{3,1,2,0:T(8,128)(2,1)S(1)} %fusion.13), channel_id=1, source_target_pairs={{0,32},{32,0},{64,96},{96,64},{128,160},{160,128},{192,224},{224,1... | collective-permute-start | bytes 589832 | tf_op jit(solution)/shard_map/ppermute | solution.py:25
  12.6 1.0 collective-permute-done
  13.7 0.1 bitcast_add_fusion
  13.8 1.9 %collective-permute-start.1 = (bf16[4,32,3,128]{3,1,2,0:T(8,128)(2,1)S(1)}, bf16[4,32,3,128]{3,1,2,0:T(8,128)(2,1)S(1)}, u32[]{:S(2)}, u32[]{:S(2)}) collective-permute-start(bf16[4,32,3,128]{3,1,2,0:T(8,128)(2,1)S(1)} %fusion.16), channel_id=1, source_target_pairs={{0,64},{32,96},{64,0},{96,32},{128,192},{160,224},{192,128},{224,1... | collective-permute-start | bytes 294920 | tf_op jit(solution)/shard_map/ppermute | solution.py:25
  15.7 0.0 copy-done.6
  15.7 0.7 broadcast_in_dim.16
  16.4 0.0 copy-start.14
  16.4 0.0 copy-start.15
  16.4 0.0 copy-start.16
  16.5 0.0 copy-start.17
  16.5 0.0 copy-start.18
  16.5 3.8 %all-to-all-start = ((bf16[16,32,128]{2,1,0:T(8,128)(2,1)}), bf16[16,32,128]{2,1,0:T(8,128)(2,1)S(1)}, u32[]{:S(2)}, u32[]{:S(2)}) async-start(bf16[16,32,128]{2,1,0:T(8,128)(2,1)} %broadcast_in_dim.16), calls=%async_computation | async-start | bytes 262144 | tf_op jit(solution)/shard_map/all_to_all | solution.py:12
  20.3 0.0 collective-permute-done.1
  20.4 3.3 %collective-permute-start.2 = (bf16[2,32,3,128]{3,1,2,0:T(8,128)(2,1)S(1)}, bf16[2,32,3,128]{3,1,2,0:T(8,128)(2,1)S(1)}, u32[]{:S(2)}, u32[]{:S(2)}) collective-permute-start(bf16[2,32,3,128]{3,1,2,0:T(8,128)(2,1)S(1)} %fusion.20), channel_id=1, source_target_pairs={{0,128},{32,160},{64,192},{96,224},{128,0},{160,32},{192,64},{224,... | collective-permute-start | bytes 147464 | tf_op jit(solution)/shard_map/ppermute | solution.py:25
  23.7 2.8 %all-to-all-done = bf16[16,32,128]{2,1,0:T(8,128)(2,1)S(1)} async-done(((bf16[16,32,128]{2,1,0:T(8,128)(2,1)}), bf16[16,32,128]{2,1,0:T(8,128)(2,1)S(1)}, u32[]{:S(2)}, u32[]{:S(2)}) %all-to-all-start) | async-done | bytes 131104 | tf_op jit(solution)/shard_map/all_to_all | solution.py:12
  26.5 1.1 convolution_convert_fusion.3
  27.6 12.7 %all-to-all-start.1 = ((bf16[32,32,128]{2,1,0:T(8,128)(2,1)}), bf16[32,32,128]{2,1,0:T(8,128)(2,1)S(1)}, u32[]{:S(2)}, u32[]{:S(2)}) async-start(bf16[32,32,128]{2,1,0:T(8,128)(2,1)} %bitcast.31), calls=%async_computation.1 | async-start | bytes 524288 | tf_op jit(solution)/shard_map/all_to_all | solution.py:12
  40.4 0.0 collective-permute-done.2
  40.4 2.8 %collective-permute-start.3 = (bf16[1,32,3,128]{3,1,2,0:T(8,128)(2,1)S(1)}, bf16[1,32,3,128]{3,1,2,0:T(8,128)(2,1)S(1)}, u32[]{:S(2)}, u32[]{:S(2)}) collective-permute-start(bf16[1,32,3,128]{3,1,2,0:T(8,128)(2,1)S(1)} %fusion.22), channel_id=1, source_target_pairs={{0,256},{32,288},{64,320},{96,352},{128,384},{160,416},{192,448},{... | collective-permute-start | bytes 73736 | tf_op jit(solution)/shard_map/ppermute | solution.py:25
  43.2 0.8 dynamic-slice_convert_fusion
  44.0 2.6 %collective-permute-done.3 = bf16[1,32,3,128]{3,1,2,0:T(8,128)(2,1)S(1)} collective-permute-done((bf16[1,32,3,128]{3,1,2,0:T(8,128)(2,1)S(1)}, bf16[1,32,3,128]{3,1,2,0:T(8,128)(2,1)S(1)}, u32[]{:S(2)}, u32[]{:S(2)}) %collective-permute-start.3) | collective-permute-done | bytes 24608 | tf_op jit(solution)/shard_map/ppermute | solution.py:25
  46.7 6.1 %all-to-all-done.1 = bf16[32,32,128]{2,1,0:T(8,128)(2,1)S(1)} async-done(((bf16[32,32,128]{2,1,0:T(8,128)(2,1)}), bf16[32,32,128]{2,1,0:T(8,128)(2,1)S(1)}, u32[]{:S(2)}, u32[]{:S(2)}) %all-to-all-start.1) | async-done | bytes 262176 | tf_op jit(solution)/shard_map/all_to_all | solution.py:12
  52.8 0.0 copy-done.5
  52.8 0.0 copy-done.7
  52.8 0.0 copy-done.8
  52.8 0.0 copy-done.13
  52.9 0.0 copy-done.14
  52.9 0.0 copy-done.15
  52.9 0.0 copy-done.16
  52.9 0.0 copy-done.17
  52.9 0.0 copy-done.18
  52.9 0.1 fusion.54
  53.0 0.0 copy-start.11
  53.0 0.0 copy-start.12
  53.1 12.0 %all_to_all.40 = bf16[16,32,128]{2,1,0:T(8,128)(2,1)S(1)} all-to-all(bf16[16,32,128]{2,1,0:T(8,128)(2,1)S(1)} %broadcast_in_dim.17), channel_id=1, replica_groups=mesh['blk'=16,'dp'=32] {'blk'}, dimensions={0} | all-to-all | bytes 262144 | tf_op jit(solution)/shard_map/all_to_all | solution.py:12
  65.1 0.5 fusion
  65.6 0.0 copy-done.1
  65.6 0.2 copy.49
  65.8 16.5 %all_to_all.41 = bf16[32,32,128]{2,1,0:T(8,128)(2,1)S(1)} all-to-all(bf16[32,32,128]{2,1,0:T(8,128)(2,1)S(1)} %bitcast.256), channel_id=1, replica_groups=mesh['blk'=16,'dp'=32] {'dp'}, dimensions={0} | all-to-all | bytes 524288 | tf_op jit(solution)/shard_map/all_to_all | solution.py:12
  82.3 0.1 fusion.52
  82.5 0.0 copy-start.9
  82.5 12.1 %all_to_all.42 = bf16[16,32,128]{2,1,0:T(8,128)(2,1)S(1)} all-to-all(bf16[16,32,128]{2,1,0:T(8,128)(2,1)S(1)} %broadcast_in_dim.18), channel_id=1, replica_groups=mesh['blk'=16,'dp'=32] {'blk'}, dimensions={0} | all-to-all | bytes 262144 | tf_op jit(solution)/shard_map/all_to_all | solution.py:12
  94.6 0.5 fusion.1
  95.0 0.2 copy.50
  95.2 15.9 %all_to_all.43 = bf16[32,32,128]{2,1,0:T(8,128)(2,1)S(1)} all-to-all(bf16[32,32,128]{2,1,0:T(8,128)(2,1)S(1)} %bitcast.257), channel_id=1, replica_groups=mesh['blk'=16,'dp'=32] {'dp'}, dimensions={0} | all-to-all | bytes 524288 | tf_op jit(solution)/shard_map/all_to_all | solution.py:12
  111.1 0.0 copy-start.10
  111.1 0.0 copy-done.11
  111.1 0.0 copy-done.12
  111.1 0.7 fusion.51
  111.9 12.0 %all_to_all.44 = bf16[16,32,128]{2,1,0:T(8,128)(2,1)S(1)} all-to-all(bf16[16,32,128]{2,1,0:T(8,128)(2,1)S(1)} %broadcast_in_dim.19), channel_id=1, replica_groups=mesh['blk'=16,'dp'=32] {'blk'}, dimensions={0} | all-to-all | bytes 262144 | tf_op jit(solution)/shard_map/all_to_all | solution.py:12
  123.9 0.5 fusion.2
  124.4 0.0 copy-done.9
  124.4 0.8 copy.51
  125.2 3.9 %all-to-all-start.7 = ((bf16[32,32,128]{2,1,0:T(8,128)(2,1)}), bf16[32,32,128]{2,1,0:T(8,128)(2,1)S(1)}, u32[]{:S(2)}, u32[]{:S(2)}) async-start(bf16[32,32,128]{2,1,0:T(8,128)(2,1)} %bitcast.44), calls=%async_computation.7 | async-start | bytes 524288 | tf_op jit(solution)/shard_map/all_to_all | solution.py:12
  129.2 2.2 %convolution_bitcast_fusion = f32[1024,512]{0,1:T(8,128)S(1)} fusion(bf16[4,1024,128]{2,1,0:T(8,128)(2,1)} %param.12, bf16[1,512,128]{2,1,0:T(8,128)(2,1)} %bitcast.260, bf16[1,512,128]{2,1,0:T(8,128)(2,1)} %bitcast.262, bf16[1,512,128]{2,1,0:T(8,128)(2,1)} %bitcast.264, bf16[1,512,128]{2,1,0:T(8,128)(2,1)} %bitcast.266), kind=kOutput, calls=%fused_computation | convolution fusion | flops 537657344 | bytes 3670016 | tf_op jit(solution)/shard_map/tpb,tcb->pc/dot_general | solution.py:110
  131.4 1.8 %copy.52 = f32[1024,512]{1,0:T(8,128)} copy(f32[1024,512]{0,1:T(8,128)S(1)} %convolution_bitcast_fusion) | data formatting | bytes 4194304
  133.2 8.3 %all-to-all-done.7 = bf16[32,32,128]{2,1,0:T(8,128)(2,1)S(1)} async-done(((bf16[32,32,128]{2,1,0:T(8,128)(2,1)}), bf16[32,32,128]{2,1,0:T(8,128)(2,1)S(1)}, u32[]{:S(2)}, u32[]{:S(2)}) %all-to-all-start.7) | async-done | bytes 262176 | tf_op jit(solution)/shard_map/all_to_all | solution.py:12
  141.6 1.6 %multiply_subtract_fusion = (f32[32,128]{1,0:T(8,128)}, f32[32,128]{1,0:T(8,128)S(1)}) fusion(f32[32,128]{1,0:T(8,128)S(1)} %convert_reduce_fusion, f32[32,128]{1,0:T(8,128)} %get-tuple-element.15, f32[4,32,128]{2,1,0:T(8,128)S(1)} %dynamic-slice_convert_fusion, f32[32,128]{1,0:T(8,128)S(1)} %copy-done.7, f32[4,32,128]{2,1,0:T(8,128)S(1)} %copy-done.5, ...), kind=kLoop, calls=%fused_computation.79 | loop fusion | flops 155648 | bytes 246144 | tf_op jit(solution)/shard_map/sub | solution.py:107
  143.2 1.4 %multiply_add_fusion = f32[32,128]{1,0:T(8,128)} fusion(f32[32,128]{1,0:T(8,128)S(1)} %convert_reduce_fusion, f32[32,128]{1,0:T(8,128)} %get-tuple-element.15, f32[32,128]{1,0:T(8,128)S(1)} %get-tuple-element.13, f32[32,128]{1,0:T(8,128)S(1)} %copy-done.7, f32[4,32,128]{2,1,0:T(8,128)S(1)} %copy-done.5, f32[32,128]{1,0:T(8,128)} %param.15, f32[32]{0:T(128)} %param.19, ...), kind=kLoop, calls=%fused_computation.80 | loop fusion | flops 61440 | bytes 115072 | tf_op jit(solution)/shard_map/add | solution.py:106
  (27 shorter events, 0.4 us)
Async XLA Ops:
  0.6 1.2 copy-start
  3.7 12.0 %copy-start.6 = (f32[32,128]{1,0:T(8,128)S(1)}, f32[32,128]{1,0:T(8,128)}, u32[]{:S(2)}) copy-start(f32[32,128]{1,0:T(8,128)} %param.22) | copy-start | bytes 49156
  3.9 9.8 %collective-permute-start = (bf16[8,32,3,128]{3,1,2,0:T(8,128)(2,1)S(1)}, bf16[8,32,3,128]{3,1,2,0:T(8,128)(2,1)S(1)}, u32[]{:S(2)}, u32[]{:S(2)}) collective-permute-start(bf16[8,32,3,128]{3,1,2,0:T(8,128)(2,1)S(1)} %fusion.13), channel_id=1, source_target_pairs={{0,32},{32,0},{64,96},{96,64},{128,160},{160,128},{192,224},{224,1... | collective-permute-start | bytes 589832 | tf_op jit(solution)/shard_map/ppermute | solution.py:25
  13.8 6.5 %collective-permute-start.1 = (bf16[4,32,3,128]{3,1,2,0:T(8,128)(2,1)S(1)}, bf16[4,32,3,128]{3,1,2,0:T(8,128)(2,1)S(1)}, u32[]{:S(2)}, u32[]{:S(2)}) collective-permute-start(bf16[4,32,3,128]{3,1,2,0:T(8,128)(2,1)S(1)} %fusion.16), channel_id=1, source_target_pairs={{0,64},{32,96},{64,0},{96,32},{128,192},{160,224},{192,128},{224,1... | collective-permute-start | bytes 294920 | tf_op jit(solution)/shard_map/ppermute | solution.py:25
  16.4 36.4 %copy-start.5 = (f32[4,32,128]{2,1,0:T(8,128)S(1)}, f32[4,32,128]{2,1,0:T(8,128)}, u32[]{:S(2)}) copy-start(f32[4,32,128]{2,1,0:T(8,128)} %param.21) | copy-start | bytes 196612
  16.4 36.4 %copy-start.7 = (f32[32,128]{1,0:T(8,128)S(1)}, f32[32,128]{1,0:T(8,128)}, u32[]{:S(2)}) copy-start(f32[32,128]{1,0:T(8,128)} %param.16) | copy-start | bytes 49156
  16.4 36.4 %copy-start.8 = (f32[32,128]{1,0:T(8,128)S(1)}, f32[32,128]{1,0:T(8,128)}, u32[]{:S(2)}) copy-start(f32[32,128]{1,0:T(8,128)} %param.15) | copy-start | bytes 49156
  16.4 36.4 %copy-start.13 = (f32[4,32,128]{2,1,0:T(8,128)S(1)}, f32[4,32,128]{2,1,0:T(8,128)}, u32[]{:S(2)}) copy-start(f32[4,32,128]{2,1,0:T(8,128)} %param.14) | copy-start | bytes 196612
  16.4 36.4 %copy-start.14 = (f32[32,128]{1,0:T(8,128)S(1)}, f32[32,128]{1,0:T(8,128)}, u32[]{:S(2)}) copy-start(f32[32,128]{1,0:T(8,128)} %param.23) | copy-start | bytes 49156
  16.4 36.4 %copy-start.15 = (f32[32]{0:T(128)S(1)}, f32[32]{0:T(128)}, u32[]{:S(2)}) copy-start(f32[32]{0:T(128)} %param.19) | copy-start | bytes 388
  16.4 36.4 %copy-start.16 = (f32[32]{0:T(128)S(1)}, f32[32]{0:T(128)}, u32[]{:S(2)}) copy-start(f32[32]{0:T(128)} %param.20) | copy-start | bytes 388
  16.5 36.4 %copy-start.17 = (f32[32]{0:T(128)S(1)}, f32[32]{0:T(128)}, u32[]{:S(2)}) copy-start(f32[32]{0:T(128)} %param.18) | copy-start | bytes 388
  16.5 36.4 %copy-start.18 = (f32[32]{0:T(128)S(1)}, f32[32]{0:T(128)}, u32[]{:S(2)}) copy-start(f32[32]{0:T(128)} %param.17) | copy-start | bytes 388
  16.5 10.0 %all-to-all-start = ((bf16[16,32,128]{2,1,0:T(8,128)(2,1)}), bf16[16,32,128]{2,1,0:T(8,128)(2,1)S(1)}, u32[]{:S(2)}, u32[]{:S(2)}) async-start(bf16[16,32,128]{2,1,0:T(8,128)(2,1)} %broadcast_in_dim.16), calls=%async_computation | async-start | bytes 262144 | tf_op jit(solution)/shard_map/all_to_all | solution.py:12
  20.4 20.0 %collective-permute-start.2 = (bf16[2,32,3,128]{3,1,2,0:T(8,128)(2,1)S(1)}, bf16[2,32,3,128]{3,1,2,0:T(8,128)(2,1)S(1)}, u32[]{:S(2)}, u32[]{:S(2)}) collective-permute-start(bf16[2,32,3,128]{3,1,2,0:T(8,128)(2,1)S(1)} %fusion.20), channel_id=1, source_target_pairs={{0,128},{32,160},{64,192},{96,224},{128,0},{160,32},{192,64},{224,... | collective-permute-start | bytes 147464 | tf_op jit(solution)/shard_map/ppermute | solution.py:25
  26.5 39.1 %copy-start.1 = (bf16[16,32,128]{2,1,0:T(8,128)(2,1)}, bf16[16,32,128]{2,1,0:T(8,128)(2,1)S(1)}, u32[]{:S(2)}) copy-start(bf16[16,32,128]{2,1,0:T(8,128)(2,1)S(1)} %all-to-all-done) | copy-start | bytes 393220
  27.6 25.1 %all-to-all-start.1 = ((bf16[32,32,128]{2,1,0:T(8,128)(2,1)}), bf16[32,32,128]{2,1,0:T(8,128)(2,1)S(1)}, u32[]{:S(2)}, u32[]{:S(2)}) async-start(bf16[32,32,128]{2,1,0:T(8,128)(2,1)} %bitcast.31), calls=%async_computation.1 | async-start | bytes 524288 | tf_op jit(solution)/shard_map/all_to_all | solution.py:12
  40.4 6.2 %collective-permute-start.3 = (bf16[1,32,3,128]{3,1,2,0:T(8,128)(2,1)S(1)}, bf16[1,32,3,128]{3,1,2,0:T(8,128)(2,1)S(1)}, u32[]{:S(2)}, u32[]{:S(2)}) collective-permute-start(bf16[1,32,3,128]{3,1,2,0:T(8,128)(2,1)S(1)} %fusion.22), channel_id=1, source_target_pairs={{0,256},{32,288},{64,320},{96,352},{128,384},{160,416},{192,448},{... | collective-permute-start | bytes 73736 | tf_op jit(solution)/shard_map/ppermute | solution.py:25
  53.0 58.1 %copy-start.11 = (f32[32,128]{1,0:T(8,128)}, f32[32,128]{1,0:T(8,128)S(1)}, u32[]{:S(2)}) copy-start(f32[32,128]{1,0:T(8,128)S(1)} %get-tuple-element.23) | copy-start | bytes 49156
  53.0 58.1 %copy-start.12 = (f32[32,128]{1,0:T(8,128)}, f32[32,128]{1,0:T(8,128)S(1)}, u32[]{:S(2)}) copy-start(f32[32,128]{1,0:T(8,128)S(1)} %get-tuple-element.25) | copy-start | bytes 49156
  65.1 64.0 %copy-start.2 = (bf16[16,32,128]{2,1,0:T(8,128)(2,1)}, bf16[16,32,128]{2,1,0:T(8,128)(2,1)S(1)}, u32[]{:S(2)}) copy-start(bf16[16,32,128]{2,1,0:T(8,128)(2,1)S(1)} %all_to_all.40) | copy-start | bytes 393220
  82.5 41.9 %copy-start.9 = (f32[32,128]{1,0:T(8,128)}, f32[32,128]{1,0:T(8,128)S(1)}, u32[]{:S(2)}) copy-start(f32[32,128]{1,0:T(8,128)S(1)} %get-tuple-element.18) | copy-start | bytes 49156
  94.6 34.6 %copy-start.3 = (bf16[16,32,128]{2,1,0:T(8,128)(2,1)}, bf16[16,32,128]{2,1,0:T(8,128)(2,1)S(1)}, u32[]{:S(2)}) copy-start(bf16[16,32,128]{2,1,0:T(8,128)(2,1)S(1)} %all_to_all.42) | copy-start | bytes 393220
  111.1 18.0 %copy-start.10 = (f32[32,128]{1,0:T(8,128)}, f32[32,128]{1,0:T(8,128)S(1)}, u32[]{:S(2)}) copy-start(f32[32,128]{1,0:T(8,128)S(1)} %convert_reduce_fusion.1) | copy-start | bytes 49156
  123.9 5.2 %copy-start.4 = (bf16[16,32,128]{2,1,0:T(8,128)(2,1)}, bf16[16,32,128]{2,1,0:T(8,128)(2,1)S(1)}, u32[]{:S(2)}) copy-start(bf16[16,32,128]{2,1,0:T(8,128)(2,1)S(1)} %all_to_all.44) | copy-start | bytes 393220
  125.2 16.3 %all-to-all-start.7 = ((bf16[32,32,128]{2,1,0:T(8,128)(2,1)}), bf16[32,32,128]{2,1,0:T(8,128)(2,1)S(1)}, u32[]{:S(2)}, u32[]{:S(2)}) async-start(bf16[32,32,128]{2,1,0:T(8,128)(2,1)} %bitcast.44), calls=%async_computation.7 | async-start | bytes 524288 | tf_op jit(solution)/shard_map/all_to_all | solution.py:12

commit v3 on v1

--- a/solution.py
+++ b/solution.py
@@ -43,18 +43,12 @@
     gain_col = adapt_gain[:, None]
     minimum_column = resting_trigger_level[:, None]
 
-    outgoing = [
-        lax.dot_general(
-            rec_weights, spikes[t], (((0,), (0,)), ((), ())), preferred_element_type=f32
-        )
-        .astype(bf16)
-        .reshape(num_blk, 1, own, trials)
-        for t in range(num_steps - 1)
-    ]
-    outgoing.append(
-        jnp.broadcast_to(volt_cot.astype(bf16), (num_blk, 1, own, trials))
-    )
-    arrived = exchange(jnp.concatenate(outgoing, axis=1), "blk")
+    sums = jnp.einsum(
+        "pc,tpb->ctb", rec_weights, spikes[: num_steps - 1], preferred_element_type=f32
+    ).astype(bf16)
+    sums = sums.reshape(num_blk, own, num_steps - 1, trials).swapaxes(1, 2)
+    copies = jnp.broadcast_to(volt_cot.astype(bf16), (num_blk, 1, own, trials))
+    arrived = exchange(jnp.concatenate([sums, copies], axis=1), "blk")
     currents = jnp.sum(arrived[:, : num_steps - 1].astype(f32), axis=0)
     pieces = arrived[:, num_steps - 1].reshape(num_blk * own, trials)
 
@@ -80,17 +74,19 @@
     for t in reversed(range(num_steps)):
         kept_pieces.insert(0, pieces)
         partials = exchange(row_partials(rec_weights, pieces, num_dp), "dp")
+        known = pulse_sensitivity[t] - threshold_values[t] * volt_adj + adapt_adj
+        volt_known = leak_rate * volt_adj + surrogates[t] * known
+        adapt_known = keep_rate * adapt_adj - gain_col * (
+            own_fired[t] * volt_adj + surrogates[t] * known
+        )
+        slope = gain_col * surrogates[t]
+        if t == 0:
+            volt_known, adapt_known, slope = lax.optimization_barrier(
+                (volt_known, adapt_known, slope)
+            )
         recurrent = jnp.sum(partials.astype(f32), axis=0)
-        spike_adj = (
-            pulse_sensitivity[t]
-            + recurrent
-            - threshold_values[t] * volt_adj
-            + adapt_adj
-        )
-        through = surrogates[t] * spike_adj
-        new_volt = leak_rate * volt_adj + through
-        adapt_adj = keep_rate * adapt_adj - gain_col * (own_fired[t] * volt_adj + through)
-        volt_adj = new_volt
+        volt_adj = volt_known + surrogates[t] * recurrent
+        adapt_adj = adapt_known - slope * recurrent
         if t > 0:
             copies = jnp.broadcast_to(volt_adj.astype(bf16), (num_blk, own, trials))
             pieces = exchange(copies, "blk").reshape(num_blk * own, trials)

time: 146 us -> 142 us (0.973)
  matrix products: 8.47 us -> 5.96 us
    dot_general x3 -> x1, matrix products: 4.31 us -> 1.87 us  [body(): jnp.einsum('pc,tpb->ctb', rec_weights, spikes[:num_steps - 1], preferred_...]
    unnamed x31 -> x41, local copies, waits for them, and re-layouts: 3.1 us -> 2.35 us
  transfers between devices with their start and end apart: 2 -> 2, of which waited for: 2 -> 2; matrix products, arithmetic and copies ran while one was open for 3% -> 4% of each run, Pallas kernels for 0% -> 0%
where the time goes in v3:
time: 142 us; the launch traced here: 139 us
  blocking collectives  87.5 us (62%)
  waiting for transfers between devices  18.6 us (13%)
  starting transfers between devices  16.7 us (12%)
  matrix products  5.96 us (4%)
  other arithmetic  4.89 us (3%)
  local copies, waits for them, and re-layouts  4.49 us (3%)
    all_to_all x6, blocking collectives, exchange(): return lax.all_to_all(parts, axis, 0, 0, tiled=True)  87.5 us
    all_to_all x2, waiting for transfers between devices, exchange(): return lax.all_to_all(parts, axis, 0, 0, tiled=True)  18.6 us
    all_to_all x2, starting transfers between devices, exchange(): return lax.all_to_all(parts, axis, 0, 0, tiled=True)  16.7 us
  transfers between devices with their start and end apart: 2, of which 2 were waited for; matrix products, arithmetic and copies ran while one was open for 4% of the time, Pallas kernels for 0%

profile of v3, /device:TPU:1, one launch (start us, length us, event | category | flops | bytes accessed | tf_op | source)
XLA Modules:
  0.0 139.2 jit_solution(12435827929800561518)
XLA Ops:
  0.6 0.0 copy-start
  0.6 0.8 convert_element_type.58
  1.5 0.4 copy-done
  1.9 1.9 %convolution_convert_fusion = bf16[512,3,128]{2,0,1:T(8,128)(2,1)S(1)} fusion(bf16[1024,512]{1,0:T(8,128)(2,1)S(1)} %copy-done, bf16[4,1024,128]{2,1,0:T(8,128)(2,1)} %param.12), kind=kOutput, calls=%fused_computation.1 | convolution fusion | flops 402849792 | bytes 2228224 | tf_op jit(solution)/shard_map/pc,tpb->ctb/dot_general | solution.py:46
  3.8 0.1 pad_maximum_fusion
  3.9 0.0 copy-start.4
  3.9 0.0 copy-start.5
  3.9 0.0 copy-start.7
  3.9 0.0 copy-start.8
  3.9 0.0 copy-start.9
  3.9 0.0 copy-start.11
  3.9 0.0 copy-start.14
  4.0 0.0 copy-start.16
  4.0 0.0 copy-start.18
  4.0 0.0 copy-start.19
  4.0 19.2 %all_to_all.40 = bf16[16,4,32,128]{3,2,1,0:T(8,128)(2,1)S(1)} all-to-all(bf16[16,4,32,128]{3,2,1,0:T(8,128)(2,1)S(1)} %pad_maximum_fusion), channel_id=1, replica_groups=mesh['blk'=16,'dp'=32] {'blk'}, dimensions={0} | all-to-all | bytes 1048576 | tf_op jit(solution)/shard_map/all_to_all | solution.py:12
  23.2 0.5 fusion
  23.7 0.8 copy.25
  24.5 12.8 %all-to-all-start.1 = ((bf16[32,32,128]{2,1,0:T(8,128)(2,1)}), bf16[32,32,128]{2,1,0:T(8,128)(2,1)S(1)}, u32[]{:S(2)}, u32[]{:S(2)}) async-start(bf16[32,32,128]{2,1,0:T(8,128)(2,1)} %bitcast.15), calls=%async_computation.1 | async-start | bytes 524288 | tf_op jit(solution)/shard_map/all_to_all | solution.py:12
  37.3 0.8 dynamic-slice_convert_fusion
  38.1 0.1 convert_reduce_fusion
  38.2 11.6 %all-to-all-done.1 = bf16[32,32,128]{2,1,0:T(8,128)(2,1)S(1)} async-done(((bf16[32,32,128]{2,1,0:T(8,128)(2,1)}), bf16[32,32,128]{2,1,0:T(8,128)(2,1)S(1)}, u32[]{:S(2)}, u32[]{:S(2)}) %all-to-all-start.1) | async-done | bytes 262176 | tf_op jit(solution)/shard_map/all_to_all | solution.py:12
  49.8 0.0 copy-done.4
  49.9 0.0 copy-done.5
  49.9 0.0 copy-done.7
  49.9 0.0 copy-done.8
  49.9 0.0 copy-done.9
  49.9 0.0 copy-done.11
  49.9 0.0 copy-done.14
  49.9 0.0 copy-done.16
  49.9 0.0 copy-done.18
  49.9 0.0 copy-done.19
  49.9 0.7 fusion.44
  50.7 12.2 %all_to_all.41 = bf16[16,32,128]{2,1,0:T(8,128)(2,1)S(1)} all-to-all(bf16[16,32,128]{2,1,0:T(8,128)(2,1)S(1)} %broadcast_in_dim.17), channel_id=1, replica_groups=mesh['blk'=16,'dp'=32] {'blk'}, dimensions={0} | all-to-all | bytes 262144 | tf_op jit(solution)/shard_map/all_to_all | solution.py:12
  62.9 0.5 fusion.1
  63.4 0.2 copy.26
  63.6 16.1 %all_to_all.42 = bf16[32,32,128]{2,1,0:T(8,128)(2,1)S(1)} all-to-all(bf16[32,32,128]{2,1,0:T(8,128)(2,1)S(1)} %bitcast.198), channel_id=1, replica_groups=mesh['blk'=16,'dp'=32] {'dp'}, dimensions={0} | all-to-all | bytes 524288 | tf_op jit(solution)/shard_map/all_to_all | solution.py:12
  79.8 0.1 fusion.42
  79.9 12.0 %all_to_all.43 = bf16[16,32,128]{2,1,0:T(8,128)(2,1)S(1)} all-to-all(bf16[16,32,128]{2,1,0:T(8,128)(2,1)S(1)} %broadcast_in_dim.18), channel_id=1, replica_groups=mesh['blk'=16,'dp'=32] {'blk'}, dimensions={0} | all-to-all | bytes 262144 | tf_op jit(solution)/shard_map/all_to_all | solution.py:12
  91.9 0.5 fusion.2
  92.4 0.2 copy.27
  92.6 15.9 %all_to_all.44 = bf16[32,32,128]{2,1,0:T(8,128)(2,1)S(1)} all-to-all(bf16[32,32,128]{2,1,0:T(8,128)(2,1)S(1)} %bitcast.199), channel_id=1, replica_groups=mesh['blk'=16,'dp'=32] {'dp'}, dimensions={0} | all-to-all | bytes 524288 | tf_op jit(solution)/shard_map/all_to_all | solution.py:12
  108.5 0.1 fusion.41
  108.6 12.0 %all_to_all.45 = bf16[16,32,128]{2,1,0:T(8,128)(2,1)S(1)} all-to-all(bf16[16,32,128]{2,1,0:T(8,128)(2,1)S(1)} %broadcast_in_dim.19), channel_id=1, replica_groups=mesh['blk'=16,'dp'=32] {'blk'}, dimensions={0} | all-to-all | bytes 262144 | tf_op jit(solution)/shard_map/all_to_all | solution.py:12
  120.7 0.5 fusion.3
  121.2 0.8 copy.28
  122.0 3.9 %all-to-all-start.7 = ((bf16[32,32,128]{2,1,0:T(8,128)(2,1)}), bf16[32,32,128]{2,1,0:T(8,128)(2,1)S(1)}, u32[]{:S(2)}, u32[]{:S(2)}) async-start(bf16[32,32,128]{2,1,0:T(8,128)(2,1)} %bitcast.28), calls=%async_computation.7 | async-start | bytes 524288 | tf_op jit(solution)/shard_map/all_to_all | solution.py:12
  125.9 0.7 multiply_subtract_fusion.1
  126.6 0.7 multiply_add_fusion.1
  127.3 0.0 copy-done.1
  127.3 0.0 copy-done.2
  127.3 0.0 copy-done.3
  127.3 2.2 %convolution_bitcast_fusion = f32[1024,512]{0,1:T(8,128)S(1)} fusion(bf16[4,1024,128]{2,1,0:T(8,128)(2,1)} %param.12, bf16[1,512,128]{2,1,0:T(8,128)(2,1)S(1)} %bitcast.201, bf16[1,512,128]{2,1,0:T(8,128)(2,1)} %bitcast.203, bf16[1,512,128]{2,1,0:T(8,128)(2,1)} %bitcast.205, bf16[1,512,128]{2,1,0:T(8,128)(2,1)} %bitcast.207), kind=kOutput, calls=%fused_computation | convolution fusion | flops 537657344 | bytes 3670016 | tf_op jit(solution)/shard_map/tpb,tcb->pc/dot_general | solution.py:93
  129.5 0.0 copy-start.6
  129.5 0.0 copy-start.10
  129.5 0.0 copy-start.12
  129.5 0.0 copy-start.13
  129.5 0.0 copy-start.15
  129.5 0.0 copy-start.17
  129.6 1.8 %copy.29 = f32[1024,512]{1,0:T(8,128)} copy(f32[1024,512]{0,1:T(8,128)S(1)} %convolution_bitcast_fusion) | data formatting | bytes 4194304
  131.4 7.0 %all-to-all-done.7 = bf16[32,32,128]{2,1,0:T(8,128)(2,1)S(1)} async-done(((bf16[32,32,128]{2,1,0:T(8,128)(2,1)}), bf16[32,32,128]{2,1,0:T(8,128)(2,1)S(1)}, u32[]{:S(2)}, u32[]{:S(2)}) %all-to-all-start.7) | async-done | bytes 262176 | tf_op jit(solution)/shard_map/all_to_all | solution.py:12
  138.4 0.0 copy-done.6
  138.4 0.0 copy-done.10
  138.5 0.7 multiply_subtract_fusion
  (17 shorter events, 0.3 us)
Async XLA Ops:
  0.6 1.2 copy-start
  3.9 46.0 %copy-start.4 = (f32[32,128]{1,0:T(8,128)S(1)}, f32[32,128]{1,0:T(8,128)}, u32[]{:S(2)}) copy-start(f32[32,128]{1,0:T(8,128)} %param.16) | copy-start | bytes 49156
  3.9 46.0 %copy-start.5 = (f32[32,128]{1,0:T(8,128)S(1)}, f32[32,128]{1,0:T(8,128)}, u32[]{:S(2)}) copy-start(f32[32,128]{1,0:T(8,128)} %param.15) | copy-start | bytes 49156
  3.9 46.0 %copy-start.7 = (f32[4,32,128]{2,1,0:T(8,128)S(1)}, f32[4,32,128]{2,1,0:T(8,128)}, u32[]{:S(2)}) copy-start(f32[4,32,128]{2,1,0:T(8,128)} %param.21) | copy-start | bytes 196612
  3.9 46.0 %copy-start.8 = (f32[32,128]{1,0:T(8,128)S(1)}, f32[32,128]{1,0:T(8,128)}, u32[]{:S(2)}) copy-start(f32[32,128]{1,0:T(8,128)} %param.22) | copy-start | bytes 49156
  3.9 46.0 %copy-start.9 = (f32[32,128]{1,0:T(8,128)S(1)}, f32[32,128]{1,0:T(8,128)}, u32[]{:S(2)}) copy-start(f32[32,128]{1,0:T(8,128)} %param.23) | copy-start | bytes 49156
  3.9 46.0 %copy-start.11 = (f32[4,32,128]{2,1,0:T(8,128)S(1)}, f32[4,32,128]{2,1,0:T(8,128)}, u32[]{:S(2)}) copy-start(f32[4,32,128]{2,1,0:T(8,128)} %param.14) | copy-start | bytes 196612
  3.9 46.0 %copy-start.14 = (f32[32]{0:T(128)S(1)}, f32[32]{0:T(128)}, u32[]{:S(2)}) copy-start(f32[32]{0:T(128)} %param.19) | copy-start | bytes 388
  4.0 46.0 %copy-start.16 = (f32[32]{0:T(128)S(1)}, f32[32]{0:T(128)}, u32[]{:S(2)}) copy-start(f32[32]{0:T(128)} %param.20) | copy-start | bytes 388
  4.0 46.0 %copy-start.18 = (f32[32]{0:T(128)S(1)}, f32[32]{0:T(128)}, u32[]{:S(2)}) copy-start(f32[32]{0:T(128)} %param.18) | copy-start | bytes 388
  4.0 46.0 %copy-start.19 = (f32[32]{0:T(128)S(1)}, f32[32]{0:T(128)}, u32[]{:S(2)}) copy-start(f32[32]{0:T(128)} %param.17) | copy-start | bytes 388
  24.5 25.3 %all-to-all-start.1 = ((bf16[32,32,128]{2,1,0:T(8,128)(2,1)}), bf16[32,32,128]{2,1,0:T(8,128)(2,1)S(1)}, u32[]{:S(2)}, u32[]{:S(2)}) async-start(bf16[32,32,128]{2,1,0:T(8,128)(2,1)} %bitcast.15), calls=%async_computation.1 | async-start | bytes 524288 | tf_op jit(solution)/shard_map/all_to_all | solution.py:12
  62.9 64.4 %copy-start.1 = (bf16[16,32,128]{2,1,0:T(8,128)(2,1)}, bf16[16,32,128]{2,1,0:T(8,128)(2,1)S(1)}, u32[]{:S(2)}) copy-start(bf16[16,32,128]{2,1,0:T(8,128)(2,1)S(1)} %all_to_all.41) | copy-start | bytes 393220
  91.9 35.4 %copy-start.2 = (bf16[16,32,128]{2,1,0:T(8,128)(2,1)}, bf16[16,32,128]{2,1,0:T(8,128)(2,1)S(1)}, u32[]{:S(2)}) copy-start(bf16[16,32,128]{2,1,0:T(8,128)(2,1)S(1)} %all_to_all.43) | copy-start | bytes 393220
  120.7 6.6 %copy-start.3 = (bf16[16,32,128]{2,1,0:T(8,128)(2,1)}, bf16[16,32,128]{2,1,0:T(8,128)(2,1)S(1)}, u32[]{:S(2)}) copy-start(bf16[16,32,128]{2,1,0:T(8,128)(2,1)S(1)} %all_to_all.45) | copy-start | bytes 393220
  122.0 16.3 %all-to-all-start.7 = ((bf16[32,32,128]{2,1,0:T(8,128)(2,1)}), bf16[32,32,128]{2,1,0:T(8,128)(2,1)S(1)}, u32[]{:S(2)}, u32[]{:S(2)}) async-start(bf16[32,32,128]{2,1,0:T(8,128)(2,1)} %bitcast.28), calls=%async_computation.7 | async-start | bytes 524288 | tf_op jit(solution)/shard_map/all_to_all | solution.py:12
  129.5 8.9 %copy-start.6 = (f32[32,128]{1,0:T(8,128)S(1)}, f32[32,128]{1,0:T(8,128)}, u32[]{:S(2)}) copy-start(f32[32,128]{1,0:T(8,128)} %param.15) | copy-start | bytes 49156
  129.5 8.9 %copy-start.10 = (f32[32,128]{1,0:T(8,128)S(1)}, f32[32,128]{1,0:T(8,128)}, u32[]{:S(2)}) copy-start(f32[32,128]{1,0:T(8,128)} %get-tuple-element.7) | copy-start | bytes 49156
  129.5 8.9 %copy-start.12 = (f32[32,128]{1,0:T(8,128)S(1)}, f32[32,128]{1,0:T(8,128)}, u32[]{:S(2)}) copy-start(f32[32,128]{1,0:T(8,128)} %get-tuple-element.8) | copy-start | bytes 49156
  129.5 8.9 %copy-start.13 = (f32[32,128]{1,0:T(8,128)S(1)}, f32[32,128]{1,0:T(8,128)}, u32[]{:S(2)}) copy-start(f32[32,128]{1,0:T(8,128)} %multiply_add_fusion.1) | copy-start | bytes 49156
  129.5 8.9 %copy-start.15 = (f32[32]{0:T(128)S(1)}, f32[32]{0:T(128)}, u32[]{:S(2)}) copy-start(f32[32]{0:T(128)} %param.19) | copy-start | bytes 388
  129.5 8.9 %copy-start.17 = (f32[32]{0:T(128)S(1)}, f32[32]{0:T(128)}, u32[]{:S(2)}) copy-start(f32[32]{0:T(128)} %param.20) | copy-start | bytes 388

commit v4 on v3

--- a/solution.py
+++ b/solution.py
@@ -43,8 +43,9 @@
     gain_col = adapt_gain[:, None]
     minimum_column = resting_trigger_level[:, None]
 
+    early = lax.optimization_barrier(spikes[: num_steps - 1])
     sums = jnp.einsum(
-        "pc,tpb->ctb", rec_weights, spikes[: num_steps - 1], preferred_element_type=f32
+        "pc,tpb->ctb", rec_weights, early, preferred_element_type=f32
     ).astype(bf16)
     sums = sums.reshape(num_blk, own, num_steps - 1, trials).swapaxes(1, 2)
     copies = jnp.broadcast_to(volt_cot.astype(bf16), (num_blk, 1, own, trials))
@@ -52,15 +53,19 @@
     currents = jnp.sum(arrived[:, : num_steps - 1].astype(f32), axis=0)
     pieces = arrived[:, num_steps - 1].reshape(num_blk * own, trials)
 
+    def threshold(adaptation):
+        return minimum_column + gain_col * adaptation
+
+    def surrogate_of(voltage, thresh):
+        return pseudo_derivative_factor / jnp.square(1.0 + jnp.abs(voltage - thresh))
+
     voltage = volt_init
     adaptation = adapt_init
     threshold_values = []
     surrogates = []
     for t in range(num_steps):
-        thresh = minimum_column + gain_col * adaptation
-        surrogates.append(
-            pseudo_derivative_factor / jnp.square(1.0 + jnp.abs(voltage - thresh))
-        )
+        thresh = threshold(adaptation)
+        surrogates.append(surrogate_of(voltage, thresh))
         threshold_values.append(thresh)
         if t + 1 < num_steps:
             voltage = (
@@ -72,20 +77,28 @@
     adapt_adj = adapt_cot
     kept_pieces = []
     for t in reversed(range(num_steps)):
+        if t == 0:
+            pieces, first_volt, first_adapt = lax.optimization_barrier(
+                (pieces, volt_init, adapt_init)
+            )
+            thresh = threshold(first_adapt)
+            surrogate = surrogate_of(first_volt, thresh)
         kept_pieces.insert(0, pieces)
         partials = exchange(row_partials(rec_weights, pieces, num_dp), "dp")
-        known = pulse_sensitivity[t] - threshold_values[t] * volt_adj + adapt_adj
-        volt_known = leak_rate * volt_adj + surrogates[t] * known
+        if t > 0:
+            thresh, surrogate = threshold_values[t], surrogates[t]
+        known = pulse_sensitivity[t] - thresh * volt_adj + adapt_adj
+        volt_known = leak_rate * volt_adj + surrogate * known
         adapt_known = keep_rate * adapt_adj - gain_col * (
-            own_fired[t] * volt_adj + surrogates[t] * known
+            own_fired[t] * volt_adj + surrogate * known
         )
-        slope = gain_col * surrogates[t]
+        slope = gain_col * surrogate
         if t == 0:
-            volt_known, adapt_known, slope = lax.optimization_barrier(
-                (volt_known, adapt_known, slope)
+            volt_known, adapt_known, surrogate, slope = lax.optimization_barrier(
+                (volt_known, adapt_known, surrogate, slope)
             )
         recurrent = jnp.sum(partials.astype(f32), axis=0)
-        volt_adj = volt_known + surrogates[t] * recurrent
+        volt_adj = volt_known + surrogate * recurrent
         adapt_adj = adapt_known - slope * recurrent
         if t > 0:
             copies = jnp.broadcast_to(volt_adj.astype(bf16), (num_blk, own, trials))

time: 142 us -> 141 us (level)
  transfers between devices with their start and end apart: 2 -> 2, of which waited for: 2 -> 2; matrix products, arithmetic and copies ran while one was open for 4% -> 5% of each run, Pallas kernels for 0% -> 0%
where the time goes in v4:
time: 141 us; the launch traced here: 138 us
  blocking collectives  87.5 us (62%)
  waiting for transfers between devices  18 us (13%)
  starting transfers between devices  16.7 us (12%)
  local copies, waits for them, and re-layouts  5.23 us (4%)
  other arithmetic  4.91 us (3%)
  matrix products  4.83 us (3%)
    all_to_all x6, blocking collectives, exchange(): return lax.all_to_all(parts, axis, 0, 0, tiled=True)  87.5 us
    all_to_all x2, waiting for transfers between devices, exchange(): return lax.all_to_all(parts, axis, 0, 0, tiled=True)  18 us
    all_to_all x2, starting transfers between devices, exchange(): return lax.all_to_all(parts, axis, 0, 0, tiled=True)  16.7 us
  transfers between devices with their start and end apart: 2, of which 2 were waited for; matrix products, arithmetic and copies ran while one was open for 5% of the time, Pallas kernels for 0%

profile of v4, /device:TPU:1, one launch (start us, length us, event | category | flops | bytes accessed | tf_op | source)
XLA Modules:
  0.0 138.1 jit_solution(11367174319874969506)
XLA Ops:
  0.6 0.0 copy-start
  0.6 0.8 convert_element_type.58
  1.5 1.2 slice.57
  2.6 0.0 copy-done
  2.7 0.7 convolution_convert_fusion
  3.5 0.1 pad_maximum_fusion
  3.5 0.0 copy-start.4
  3.5 0.0 copy-start.5
  3.5 0.0 copy-start.6
  3.6 0.0 copy-start.10
  3.6 0.0 copy-start.11
  3.6 0.0 copy-start.12
  3.6 0.0 copy-start.13
  3.6 0.0 copy-start.14
  3.6 0.0 copy-start.15
  3.6 0.0 copy-start.16
  3.6 19.2 %all_to_all.40 = bf16[16,4,32,128]{3,2,1,0:T(8,128)(2,1)S(1)} all-to-all(bf16[16,4,32,128]{3,2,1,0:T(8,128)(2,1)S(1)} %pad_maximum_fusion), channel_id=1, replica_groups=mesh['blk'=16,'dp'=32] {'blk'}, dimensions={0} | all-to-all | bytes 1048576 | tf_op jit(solution)/shard_map/all_to_all | solution.py:12
  22.8 0.5 fusion
  23.3 0.8 copy.25
  24.1 12.8 %all-to-all-start.1 = ((bf16[32,32,128]{2,1,0:T(8,128)(2,1)}), bf16[32,32,128]{2,1,0:T(8,128)(2,1)S(1)}, u32[]{:S(2)}, u32[]{:S(2)}) async-start(bf16[32,32,128]{2,1,0:T(8,128)(2,1)} %bitcast.15), calls=%async_computation.1 | async-start | bytes 524288 | tf_op jit(solution)/shard_map/all_to_all | solution.py:12
  37.0 0.8 dynamic-slice_convert_fusion
  37.7 0.1 convert_reduce_fusion
  37.8 11.6 %all-to-all-done.1 = bf16[32,32,128]{2,1,0:T(8,128)(2,1)S(1)} async-done(((bf16[32,32,128]{2,1,0:T(8,128)(2,1)}), bf16[32,32,128]{2,1,0:T(8,128)(2,1)S(1)}, u32[]{:S(2)}, u32[]{:S(2)}) %all-to-all-start.1) | async-done | bytes 262176 | tf_op jit(solution)/shard_map/all_to_all | solution.py:12
  49.5 0.0 copy-done.4
  49.5 0.0 copy-done.5
  49.5 0.0 copy-done.6
  49.5 0.0 copy-done.10
  49.5 0.0 copy-done.11
  49.5 0.0 copy-done.12
  49.5 0.0 copy-done.13
  49.6 0.0 copy-done.14
  49.6 0.0 copy-done.15
  49.6 0.0 copy-done.16
  49.6 0.1 fusion.43
  49.7 12.2 %all_to_all.41 = bf16[16,32,128]{2,1,0:T(8,128)(2,1)S(1)} all-to-all(bf16[16,32,128]{2,1,0:T(8,128)(2,1)S(1)} %broadcast_in_dim.17), channel_id=1, replica_groups=mesh['blk'=16,'dp'=32] {'blk'}, dimensions={0} | all-to-all | bytes 262144 | tf_op jit(solution)/shard_map/all_to_all | solution.py:12
  61.9 0.5 fusion.1
  62.4 0.2 copy.26
  62.6 16.2 %all_to_all.42 = bf16[32,32,128]{2,1,0:T(8,128)(2,1)S(1)} all-to-all(bf16[32,32,128]{2,1,0:T(8,128)(2,1)S(1)} %bitcast.199), channel_id=1, replica_groups=mesh['blk'=16,'dp'=32] {'dp'}, dimensions={0} | all-to-all | bytes 524288 | tf_op jit(solution)/shard_map/all_to_all | solution.py:12
  78.8 0.1 fusion.41
  79.0 12.0 %all_to_all.43 = bf16[16,32,128]{2,1,0:T(8,128)(2,1)S(1)} all-to-all(bf16[16,32,128]{2,1,0:T(8,128)(2,1)S(1)} %broadcast_in_dim.18), channel_id=1, replica_groups=mesh['blk'=16,'dp'=32] {'blk'}, dimensions={0} | all-to-all | bytes 262144 | tf_op jit(solution)/shard_map/all_to_all | solution.py:12
  91.0 0.5 fusion.2
  91.5 0.2 copy.27
  91.7 15.9 %all_to_all.44 = bf16[32,32,128]{2,1,0:T(8,128)(2,1)S(1)} all-to-all(bf16[32,32,128]{2,1,0:T(8,128)(2,1)S(1)} %bitcast.200), channel_id=1, replica_groups=mesh['blk'=16,'dp'=32] {'dp'}, dimensions={0} | all-to-all | bytes 524288 | tf_op jit(solution)/shard_map/all_to_all | solution.py:12
  107.6 0.1 fusion.40
  107.7 12.0 %all_to_all.45 = bf16[16,32,128]{2,1,0:T(8,128)(2,1)S(1)} all-to-all(bf16[16,32,128]{2,1,0:T(8,128)(2,1)S(1)} %broadcast_in_dim.19), channel_id=1, replica_groups=mesh['blk'=16,'dp'=32] {'blk'}, dimensions={0} | all-to-all | bytes 262144 | tf_op jit(solution)/shard_map/all_to_all | solution.py:12
  119.8 0.5 fusion.3
  120.3 0.8 copy.28
  121.1 3.9 %all-to-all-start.7 = ((bf16[32,32,128]{2,1,0:T(8,128)(2,1)}), bf16[32,32,128]{2,1,0:T(8,128)(2,1)S(1)}, u32[]{:S(2)}, u32[]{:S(2)}) async-start(bf16[32,32,128]{2,1,0:T(8,128)(2,1)} %bitcast.28), calls=%async_computation.7 | async-start | bytes 524288 | tf_op jit(solution)/shard_map/all_to_all | solution.py:12
  125.0 0.7 broadcast_multiply_fusion
  125.7 0.7 multiply_subtract_fusion.1
  126.4 0.7 multiply_add_fusion.2
  127.1 0.0 copy-done.1
  127.1 0.0 copy-done.2
  127.1 0.0 copy-done.3
  127.1 2.2 %convolution_bitcast_fusion = f32[1024,512]{0,1:T(8,128)S(1)} fusion(bf16[4,1024,128]{2,1,0:T(8,128)(2,1)} %param.12, bf16[1,512,128]{2,1,0:T(8,128)(2,1)S(1)} %bitcast.202, bf16[1,512,128]{2,1,0:T(8,128)(2,1)} %bitcast.204, bf16[1,512,128]{2,1,0:T(8,128)(2,1)} %bitcast.206, bf16[1,512,128]{2,1,0:T(8,128)(2,1)} %bitcast.208), kind=kOutput, calls=%fused_computation | convolution fusion | flops 537657344 | bytes 3670016 | tf_op jit(solution)/shard_map/tpb,tcb->pc/dot_general | solution.py:106
  129.2 0.0 copy-start.7
  129.3 0.0 copy-start.8
  129.3 0.0 copy-start.9
  129.3 1.8 %copy.29 = f32[1024,512]{1,0:T(8,128)} copy(f32[1024,512]{0,1:T(8,128)S(1)} %convolution_bitcast_fusion) | data formatting | bytes 4194304
  131.1 6.3 %all-to-all-done.7 = bf16[32,32,128]{2,1,0:T(8,128)(2,1)S(1)} async-done(((bf16[32,32,128]{2,1,0:T(8,128)(2,1)}), bf16[32,32,128]{2,1,0:T(8,128)(2,1)S(1)}, u32[]{:S(2)}, u32[]{:S(2)}) %all-to-all-start.7) | async-done | bytes 262176 | tf_op jit(solution)/shard_map/all_to_all | solution.py:12
  137.5 0.0 copy-done.7
  137.5 0.0 copy-done.8
  137.5 0.0 copy-done.9
  137.5 0.6 multiply_subtract_fusion
  (13 shorter events, 0.3 us)
Async XLA Ops:
  0.6 2.0 %copy-start = (bf16[1024,512]{1,0:T(8,128)(2,1)S(1)}, bf16[1024,512]{1,0:T(8,128)(2,1)}, u32[]{:S(2)}) copy-start(bf16[1024,512]{1,0:T(8,128)(2,1)} %param.13) | copy-start | bytes 3145732
  3.5 46.0 %copy-start.4 = (f32[32,128]{1,0:T(8,128)S(1)}, f32[32,128]{1,0:T(8,128)}, u32[]{:S(2)}) copy-start(f32[32,128]{1,0:T(8,128)} %param.16) | copy-start | bytes 49156
  3.5 46.0 %copy-start.5 = (f32[4,32,128]{2,1,0:T(8,128)S(1)}, f32[4,32,128]{2,1,0:T(8,128)}, u32[]{:S(2)}) copy-start(f32[4,32,128]{2,1,0:T(8,128)} %param.21) | copy-start | bytes 196612
  3.5 46.0 %copy-start.6 = (f32[32,128]{1,0:T(8,128)S(1)}, f32[32,128]{1,0:T(8,128)}, u32[]{:S(2)}) copy-start(f32[32,128]{1,0:T(8,128)} %param.22) | copy-start | bytes 49156
  3.6 46.0 %copy-start.10 = (f32[4,32,128]{2,1,0:T(8,128)S(1)}, f32[4,32,128]{2,1,0:T(8,128)}, u32[]{:S(2)}) copy-start(f32[4,32,128]{2,1,0:T(8,128)} %param.14) | copy-start | bytes 196612
  3.6 46.0 %copy-start.11 = (f32[32,128]{1,0:T(8,128)S(1)}, f32[32,128]{1,0:T(8,128)}, u32[]{:S(2)}) copy-start(f32[32,128]{1,0:T(8,128)} %param.23) | copy-start | bytes 49156
  3.6 46.0 %copy-start.12 = (f32[32,128]{1,0:T(8,128)S(1)}, f32[32,128]{1,0:T(8,128)}, u32[]{:S(2)}) copy-start(f32[32,128]{1,0:T(8,128)} %param.15) | copy-start | bytes 49156
  3.6 46.0 %copy-start.13 = (f32[32]{0:T(128)S(1)}, f32[32]{0:T(128)}, u32[]{:S(2)}) copy-start(f32[32]{0:T(128)} %param.19) | copy-start | bytes 388
  3.6 46.0 %copy-start.14 = (f32[32]{0:T(128)S(1)}, f32[32]{0:T(128)}, u32[]{:S(2)}) copy-start(f32[32]{0:T(128)} %param.20) | copy-start | bytes 388
  3.6 46.0 %copy-start.15 = (f32[32]{0:T(128)S(1)}, f32[32]{0:T(128)}, u32[]{:S(2)}) copy-start(f32[32]{0:T(128)} %param.18) | copy-start | bytes 388
  3.6 46.0 %copy-start.16 = (f32[32]{0:T(128)S(1)}, f32[32]{0:T(128)}, u32[]{:S(2)}) copy-start(f32[32]{0:T(128)} %param.17) | copy-start | bytes 388
  24.1 25.3 %all-to-all-start.1 = ((bf16[32,32,128]{2,1,0:T(8,128)(2,1)}), bf16[32,32,128]{2,1,0:T(8,128)(2,1)S(1)}, u32[]{:S(2)}, u32[]{:S(2)}) async-start(bf16[32,32,128]{2,1,0:T(8,128)(2,1)} %bitcast.15), calls=%async_computation.1 | async-start | bytes 524288 | tf_op jit(solution)/shard_map/all_to_all | solution.py:12
  61.9 65.1 %copy-start.1 = (bf16[16,32,128]{2,1,0:T(8,128)(2,1)}, bf16[16,32,128]{2,1,0:T(8,128)(2,1)S(1)}, u32[]{:S(2)}) copy-start(bf16[16,32,128]{2,1,0:T(8,128)(2,1)S(1)} %all_to_all.41) | copy-start | bytes 393220
  91.0 36.0 %copy-start.2 = (bf16[16,32,128]{2,1,0:T(8,128)(2,1)}, bf16[16,32,128]{2,1,0:T(8,128)(2,1)S(1)}, u32[]{:S(2)}) copy-start(bf16[16,32,128]{2,1,0:T(8,128)(2,1)S(1)} %all_to_all.43) | copy-start | bytes 393220
  119.8 7.3 %copy-start.3 = (bf16[16,32,128]{2,1,0:T(8,128)(2,1)}, bf16[16,32,128]{2,1,0:T(8,128)(2,1)S(1)}, u32[]{:S(2)}) copy-start(bf16[16,32,128]{2,1,0:T(8,128)(2,1)S(1)} %all_to_all.45) | copy-start | bytes 393220
  121.1 16.3 %all-to-all-start.7 = ((bf16[32,32,128]{2,1,0:T(8,128)(2,1)}), bf16[32,32,128]{2,1,0:T(8,128)(2,1)S(1)}, u32[]{:S(2)}, u32[]{:S(2)}) async-start(bf16[32,32,128]{2,1,0:T(8,128)(2,1)} %bitcast.28), calls=%async_computation.7 | async-start | bytes 524288 | tf_op jit(solution)/shard_map/all_to_all | solution.py:12
  129.2 8.2 %copy-start.7 = (f32[32,128]{1,0:T(8,128)S(1)}, f32[32,128]{1,0:T(8,128)}, u32[]{:S(2)}) copy-start(f32[32,128]{1,0:T(8,128)} %get-tuple-element.15) | copy-start | bytes 49156
  129.3 8.2 %copy-start.8 = (f32[32,128]{1,0:T(8,128)S(1)}, f32[32,128]{1,0:T(8,128)}, u32[]{:S(2)}) copy-start(f32[32,128]{1,0:T(8,128)} %multiply_add_fusion.2) | copy-start | bytes 49156
  129.3 8.2 %copy-start.9 = (f32[32,128]{1,0:T(8,128)S(1)}, f32[32,128]{1,0:T(8,128)}, u32[]{:S(2)}) copy-start(f32[32,128]{1,0:T(8,128)} %get-tuple-element.16) | copy-start | bytes 49156

commit v5 on v4

--- a/solution.py
+++ b/solution.py
@@ -13,8 +13,13 @@
 
 
 def row_partials(weights, pieces, num_dp):
-    part = jnp.dot(weights, pieces, preferred_element_type=f32).astype(bf16)
-    return part.reshape(num_dp, -1, part.shape[-1])
+    rows, cols = weights.shape
+    return jnp.einsum(
+        "kpc,cb->kpb",
+        weights.reshape(num_dp, rows // num_dp, cols),
+        pieces,
+        preferred_element_type=f32,
+    ).astype(bf16)
 
 
 def body(
@@ -47,8 +52,9 @@
     sums = jnp.einsum(
         "pc,tpb->ctb", rec_weights, early, preferred_element_type=f32
     ).astype(bf16)
+    sums, last_adj = lax.optimization_barrier((sums, volt_cot))
     sums = sums.reshape(num_blk, own, num_steps - 1, trials).swapaxes(1, 2)
-    copies = jnp.broadcast_to(volt_cot.astype(bf16), (num_blk, 1, own, trials))
+    copies = jnp.broadcast_to(last_adj.astype(bf16), (num_blk, 1, own, trials))
     arrived = exchange(jnp.concatenate([sums, copies], axis=1), "blk")
     currents = jnp.sum(arrived[:, : num_steps - 1].astype(f32), axis=0)
     pieces = arrived[:, num_steps - 1].reshape(num_blk * own, trials)

time: 141 us -> 139 us (0.986)
  local copies, waits for them, and re-layouts: 5.23 us -> 3.47 us
    convert_element_type x4 -> x0, local copies, waits for them, and re-layouts: 2.02 us -> none  [row_partials(): part = jnp.dot(weights, pieces, preferred_element_type=f32).astype(bf16)]
where the time goes in v5:
time: 139 us; the launch traced here: 137 us
  blocking collectives  87.5 us (63%)
  waiting for transfers between devices  18 us (13%)
  starting transfers between devices  16.7 us (12%)
  matrix products  6.07 us (4%)
  other arithmetic  4.1 us (3%)
  local copies, waits for them, and re-layouts  3.47 us (2%)
    all_to_all x6, blocking collectives, exchange(): return lax.all_to_all(parts, axis, 0, 0, tiled=True)  87.5 us
    all_to_all x2, waiting for transfers between devices, exchange(): return lax.all_to_all(parts, axis, 0, 0, tiled=True)  18 us
    all_to_all x2, starting transfers between devices, exchange(): return lax.all_to_all(parts, axis, 0, 0, tiled=True)  16.7 us
    dot_general x4, matrix products, row_partials(): jnp.einsum('kpc,cb->kpb', weights.reshape(num_dp, rows // num_dp, cols),...  3.16 us
  transfers between devices with their start and end apart: 2, of which 2 were waited for; matrix products, arithmetic and copies ran while one was open for 5% of the time, Pallas kernels for 0%

profile of v5, /device:TPU:1, one launch (start us, length us, event | category | flops | bytes accessed | tf_op | source)
XLA Modules:
  0.0 136.8 jit_solution(2033912177427937317)
XLA Ops:
  0.6 0.0 copy-start
  0.6 1.3 slice.57
  1.9 0.2 copy-done
  2.1 0.0 copy-start.3
  2.1 0.7 convolution_convert_fusion
  2.9 0.0 copy-done.3
  2.9 0.1 pad_maximum_fusion
  3.0 0.0 copy-start.1
  3.0 0.0 copy-start.2
  3.0 0.0 copy-start.10
  3.0 0.0 copy-start.11
  3.0 0.0 copy-start.12
  3.0 0.0 copy-start.13
  3.1 0.0 copy-start.14
  3.1 0.0 copy-start.15
  3.1 0.0 copy-start.16
  3.1 19.2 %all_to_all.40 = bf16[16,4,32,128]{3,2,1,0:T(8,128)(2,1)S(1)} all-to-all(bf16[16,4,32,128]{3,2,1,0:T(8,128)(2,1)S(1)} %pad_maximum_fusion), channel_id=1, replica_groups=mesh['blk'=16,'dp'=32] {'blk'}, dimensions={0} | all-to-all | bytes 1048576 | tf_op jit(solution)/shard_map/all_to_all | solution.py:12
  22.3 1.1 fusion
  23.4 12.8 %all-to-all-start.1 = ((bf16[32,32,128]{2,1,0:T(8,128)(2,1)}), bf16[32,32,128]{2,1,0:T(8,128)(2,1)S(1)}, u32[]{:S(2)}, u32[]{:S(2)}) async-start(bf16[32,32,128]{2,1,0:T(8,128)(2,1)} %fusion), calls=%async_computation.1 | async-start | bytes 524288 | tf_op jit(solution)/shard_map/all_to_all | solution.py:12
  36.2 0.8 dynamic-slice_convert_fusion
  37.0 0.1 convert_reduce_fusion
  37.1 11.6 %all-to-all-done.1 = bf16[32,32,128]{2,1,0:T(8,128)(2,1)S(1)} async-done(((bf16[32,32,128]{2,1,0:T(8,128)(2,1)}), bf16[32,32,128]{2,1,0:T(8,128)(2,1)S(1)}, u32[]{:S(2)}, u32[]{:S(2)}) %all-to-all-start.1) | async-done | bytes 262176 | tf_op jit(solution)/shard_map/all_to_all | solution.py:12
  48.8 0.0 copy-done.1
  48.8 0.0 copy-done.2
  48.8 0.0 copy-done.10
  48.8 0.0 copy-done.11
  48.8 0.0 copy-done.12
  48.8 0.0 copy-done.13
  48.8 0.0 copy-done.14
  48.8 0.0 copy-done.15
  48.8 0.0 copy-done.16
  48.9 0.1 fusion.44
  49.0 12.2 %all_to_all.41 = bf16[16,32,128]{2,1,0:T(8,128)(2,1)S(1)} all-to-all(bf16[16,32,128]{2,1,0:T(8,128)(2,1)S(1)} %broadcast_in_dim.17), channel_id=1, replica_groups=mesh['blk'=16,'dp'=32] {'blk'}, dimensions={0} | all-to-all | bytes 262144 | tf_op jit(solution)/shard_map/all_to_all | solution.py:12
  61.2 0.0 copy-start.4
  61.2 0.4 fusion.1
  61.7 16.1 %all_to_all.42 = bf16[32,32,128]{2,1,0:T(8,128)(2,1)S(1)} all-to-all(bf16[32,32,128]{2,1,0:T(8,128)(2,1)S(1)} %fusion.1), channel_id=1, replica_groups=mesh['blk'=16,'dp'=32] {'dp'}, dimensions={0} | all-to-all | bytes 524288 | tf_op jit(solution)/shard_map/all_to_all | solution.py:12
  77.9 0.1 fusion.42
  78.0 12.0 %all_to_all.43 = bf16[16,32,128]{2,1,0:T(8,128)(2,1)S(1)} all-to-all(bf16[16,32,128]{2,1,0:T(8,128)(2,1)S(1)} %broadcast_in_dim.18), channel_id=1, replica_groups=mesh['blk'=16,'dp'=32] {'blk'}, dimensions={0} | all-to-all | bytes 262144 | tf_op jit(solution)/shard_map/all_to_all | solution.py:12
  90.0 0.0 copy-start.5
  90.0 0.4 fusion.2
  90.5 15.9 %all_to_all.44 = bf16[32,32,128]{2,1,0:T(8,128)(2,1)S(1)} all-to-all(bf16[32,32,128]{2,1,0:T(8,128)(2,1)S(1)} %fusion.2), channel_id=1, replica_groups=mesh['blk'=16,'dp'=32] {'dp'}, dimensions={0} | all-to-all | bytes 524288 | tf_op jit(solution)/shard_map/all_to_all | solution.py:12
  106.4 0.1 fusion.41
  106.5 12.0 %all_to_all.45 = bf16[16,32,128]{2,1,0:T(8,128)(2,1)S(1)} all-to-all(bf16[16,32,128]{2,1,0:T(8,128)(2,1)S(1)} %broadcast_in_dim.19), channel_id=1, replica_groups=mesh['blk'=16,'dp'=32] {'blk'}, dimensions={0} | all-to-all | bytes 262144 | tf_op jit(solution)/shard_map/all_to_all | solution.py:12
  118.6 0.0 copy-start.6
  118.6 1.1 fusion.3
  119.7 3.9 %all-to-all-start.7 = ((bf16[32,32,128]{2,1,0:T(8,128)(2,1)}), bf16[32,32,128]{2,1,0:T(8,128)(2,1)S(1)}, u32[]{:S(2)}, u32[]{:S(2)}) async-start(bf16[32,32,128]{2,1,0:T(8,128)(2,1)} %fusion.3), calls=%async_computation.7 | async-start | bytes 524288 | tf_op jit(solution)/shard_map/all_to_all | solution.py:12
  123.6 0.7 broadcast_multiply_fusion
  124.3 0.7 multiply_subtract_fusion.1
  125.0 0.7 multiply_add_fusion.2
  125.7 0.0 copy-done.4
  125.7 0.0 copy-done.5
  125.7 0.0 copy-done.6
  125.7 2.2 %convolution_bitcast_fusion = f32[1024,512]{0,1:T(8,128)S(1)} fusion(bf16[4,1024,128]{2,1,0:T(8,128)(2,1)} %param.12, bf16[1,512,128]{2,1,0:T(8,128)(2,1)S(1)} %bitcast.210, bf16[1,512,128]{2,1,0:T(8,128)(2,1)} %bitcast.212, bf16[1,512,128]{2,1,0:T(8,128)(2,1)} %bitcast.214, bf16[1,512,128]{2,1,0:T(8,128)(2,1)} %bitcast.216), kind=kOutput, calls=%fused_computation | convolution fusion | flops 537657344 | bytes 3670016 | tf_op jit(solution)/shard_map/tpb,tcb->pc/dot_general | solution.py:112
  127.9 0.0 copy-start.7
  127.9 0.0 copy-start.8
  127.9 0.0 copy-start.9
  127.9 1.8 %copy.19 = f32[1024,512]{1,0:T(8,128)} copy(f32[1024,512]{0,1:T(8,128)S(1)} %convolution_bitcast_fusion) | data formatting | bytes 4194304
  129.7 6.3 %all-to-all-done.7 = bf16[32,32,128]{2,1,0:T(8,128)(2,1)S(1)} async-done(((bf16[32,32,128]{2,1,0:T(8,128)(2,1)}), bf16[32,32,128]{2,1,0:T(8,128)(2,1)S(1)}, u32[]{:S(2)}, u32[]{:S(2)}) %all-to-all-start.7) | async-done | bytes 262176 | tf_op jit(solution)/shard_map/all_to_all | solution.py:12
  136.1 0.0 copy-done.7
  136.1 0.0 copy-done.8
  136.1 0.0 copy-done.9
  136.1 0.6 multiply_subtract_fusion
  (11 shorter events, 0.3 us)
Async XLA Ops:
  0.6 1.5 %copy-start = (bf16[1024,512]{1,0:T(8,128)(2,1)S(1)}, bf16[1024,512]{1,0:T(8,128)(2,1)}, u32[]{:S(2)}) copy-start(bf16[1024,512]{1,0:T(8,128)(2,1)} %param.13) | copy-start | bytes 3145732
  2.1 0.8 copy-start.3
  3.0 45.8 %copy-start.1 = (f32[32,128]{1,0:T(8,128)S(1)}, f32[32,128]{1,0:T(8,128)}, u32[]{:S(2)}) copy-start(f32[32,128]{1,0:T(8,128)} %param.16) | copy-start | bytes 49156
  3.0 45.8 %copy-start.2 = (f32[4,32,128]{2,1,0:T(8,128)S(1)}, f32[4,32,128]{2,1,0:T(8,128)}, u32[]{:S(2)}) copy-start(f32[4,32,128]{2,1,0:T(8,128)} %param.21) | copy-start | bytes 196612
  3.0 45.8 %copy-start.10 = (f32[4,32,128]{2,1,0:T(8,128)S(1)}, f32[4,32,128]{2,1,0:T(8,128)}, u32[]{:S(2)}) copy-start(f32[4,32,128]{2,1,0:T(8,128)} %param.14) | copy-start | bytes 196612
  3.0 45.8 %copy-start.11 = (f32[32,128]{1,0:T(8,128)S(1)}, f32[32,128]{1,0:T(8,128)}, u32[]{:S(2)}) copy-start(f32[32,128]{1,0:T(8,128)} %param.23) | copy-start | bytes 49156
  3.0 45.8 %copy-start.12 = (f32[32,128]{1,0:T(8,128)S(1)}, f32[32,128]{1,0:T(8,128)}, u32[]{:S(2)}) copy-start(f32[32,128]{1,0:T(8,128)} %param.15) | copy-start | bytes 49156
  3.0 45.8 %copy-start.13 = (f32[32]{0:T(128)S(1)}, f32[32]{0:T(128)}, u32[]{:S(2)}) copy-start(f32[32]{0:T(128)} %param.19) | copy-start | bytes 388
  3.1 45.8 %copy-start.14 = (f32[32]{0:T(128)S(1)}, f32[32]{0:T(128)}, u32[]{:S(2)}) copy-start(f32[32]{0:T(128)} %param.20) | copy-start | bytes 388
  3.1 45.8 %copy-start.15 = (f32[32]{0:T(128)S(1)}, f32[32]{0:T(128)}, u32[]{:S(2)}) copy-start(f32[32]{0:T(128)} %param.18) | copy-start | bytes 388
  3.1 45.8 %copy-start.16 = (f32[32]{0:T(128)S(1)}, f32[32]{0:T(128)}, u32[]{:S(2)}) copy-start(f32[32]{0:T(128)} %param.17) | copy-start | bytes 388
  23.4 25.3 %all-to-all-start.1 = ((bf16[32,32,128]{2,1,0:T(8,128)(2,1)}), bf16[32,32,128]{2,1,0:T(8,128)(2,1)S(1)}, u32[]{:S(2)}, u32[]{:S(2)}) async-start(bf16[32,32,128]{2,1,0:T(8,128)(2,1)} %fusion), calls=%async_computation.1 | async-start | bytes 524288 | tf_op jit(solution)/shard_map/all_to_all | solution.py:12
  61.2 64.5 %copy-start.4 = (bf16[16,32,128]{2,1,0:T(8,128)(2,1)}, bf16[16,32,128]{2,1,0:T(8,128)(2,1)S(1)}, u32[]{:S(2)}) copy-start(bf16[16,32,128]{2,1,0:T(8,128)(2,1)S(1)} %all_to_all.41) | copy-start | bytes 393220
  90.0 35.6 %copy-start.5 = (bf16[16,32,128]{2,1,0:T(8,128)(2,1)}, bf16[16,32,128]{2,1,0:T(8,128)(2,1)S(1)}, u32[]{:S(2)}) copy-start(bf16[16,32,128]{2,1,0:T(8,128)(2,1)S(1)} %all_to_all.43) | copy-start | bytes 393220
  118.6 7.1 %copy-start.6 = (bf16[16,32,128]{2,1,0:T(8,128)(2,1)}, bf16[16,32,128]{2,1,0:T(8,128)(2,1)S(1)}, u32[]{:S(2)}) copy-start(bf16[16,32,128]{2,1,0:T(8,128)(2,1)S(1)} %all_to_all.45) | copy-start | bytes 393220
  119.7 16.3 %all-to-all-start.7 = ((bf16[32,32,128]{2,1,0:T(8,128)(2,1)}), bf16[32,32,128]{2,1,0:T(8,128)(2,1)S(1)}, u32[]{:S(2)}, u32[]{:S(2)}) async-start(bf16[32,32,128]{2,1,0:T(8,128)(2,1)} %fusion.3), calls=%async_computation.7 | async-start | bytes 524288 | tf_op jit(solution)/shard_map/all_to_all | solution.py:12
  127.9 8.2 %copy-start.7 = (f32[32,128]{1,0:T(8,128)S(1)}, f32[32,128]{1,0:T(8,128)}, u32[]{:S(2)}) copy-start(f32[32,128]{1,0:T(8,128)} %get-tuple-element.19) | copy-start | bytes 49156
  127.9 8.2 %copy-start.8 = (f32[32,128]{1,0:T(8,128)S(1)}, f32[32,128]{1,0:T(8,128)}, u32[]{:S(2)}) copy-start(f32[32,128]{1,0:T(8,128)} %multiply_add_fusion.2) | copy-start | bytes 49156
  127.9 8.2 %copy-start.9 = (f32[32,128]{1,0:T(8,128)S(1)}, f32[32,128]{1,0:T(8,128)}, u32[]{:S(2)}) copy-start(f32[32,128]{1,0:T(8,128)} %get-tuple-element.20) | copy-start | bytes 49156

commit v6 on v5

--- a/solution.py
+++ b/solution.py
@@ -8,18 +8,34 @@
 f32 = jnp.float32
 
 
+def leader(axis):
+    size = lax.axis_size(axis)
+    return size * 5 // 8 if axis == "dp" else size * 11 // 16
+
+
+def rotated(parts, start):
+    return jnp.concatenate([parts[start:], parts[:start]], axis=0)
+
+
 def exchange(parts, axis):
-    return lax.all_to_all(parts, axis, 0, 0, tiled=True)
+    size = lax.axis_size(axis)
+    order = [(leader(axis) + p) % size for p in range(size)]
+    return lax.all_to_all(parts, axis, 0, 0, axis_index_groups=[order], tiled=True)
+
+
+def by_member(parts, axis):
+    return rotated(parts, lax.axis_size(axis) - leader(axis))
 
 
 def row_partials(weights, pieces, num_dp):
     rows, cols = weights.shape
-    return jnp.einsum(
+    part = jnp.einsum(
         "kpc,cb->kpb",
         weights.reshape(num_dp, rows // num_dp, cols),
         pieces,
         preferred_element_type=f32,
     ).astype(bf16)
+    return rotated(part, leader("dp"))
 
 
 def body(
@@ -54,10 +70,11 @@
     ).astype(bf16)
     sums, last_adj = lax.optimization_barrier((sums, volt_cot))
     sums = sums.reshape(num_blk, own, num_steps - 1, trials).swapaxes(1, 2)
+    sums = rotated(sums, leader("blk"))
     copies = jnp.broadcast_to(last_adj.astype(bf16), (num_blk, 1, own, trials))
     arrived = exchange(jnp.concatenate([sums, copies], axis=1), "blk")
     currents = jnp.sum(arrived[:, : num_steps - 1].astype(f32), axis=0)
-    pieces = arrived[:, num_steps - 1].reshape(num_blk * own, trials)
+    pieces = by_member(arrived[:, num_steps - 1], "blk").reshape(num_blk * own, trials)
 
     def threshold(adaptation):
         return minimum_column + gain_col * adaptation
@@ -108,7 +125,8 @@
         adapt_adj = adapt_known - slope * recurrent
         if t > 0:
             copies = jnp.broadcast_to(volt_adj.astype(bf16), (num_blk, own, trials))
-            pieces = exchange(copies, "blk").reshape(num_blk * own, trials)
+            pieces = by_member(exchange(copies, "blk"), "blk")
+            pieces = pieces.reshape(num_blk * own, trials)
     weight_sum = jnp.einsum(
         "tpb,tcb->pc", spikes, jnp.stack(kept_pieces), preferred_element_type=f32
     )

time: 139 us -> 130 us (0.935); the launches traced: 137 us -> 130 us
  waiting for transfers between devices: 18 us -> 6.25 us
  starting transfers between devices: 16.7 us -> 25.6 us
  blocking collectives: 87.5 us -> 82.9 us
  other arithmetic: 4.1 us -> 5.69 us
  matrix products: 6.07 us -> 4.66 us
    all_to_all x2, waiting for transfers between devices: 18 us -> 6.25 us  [exchange(): lax.all_to_all(parts, axis, 0, 0, axis_index_groups=[order], tiled=True)]
    all_to_all x2, starting transfers between devices: 16.7 us -> 25.6 us  [exchange(): lax.all_to_all(parts, axis, 0, 0, axis_index_groups=[order], tiled=True)]
    all_to_all x6, blocking collectives: 87.5 us -> 82.9 us  [exchange(): lax.all_to_all(parts, axis, 0, 0, axis_index_groups=[order], tiled=True)]
    concatenate x0 -> x8, other arithmetic: none -> 1.57 us  [rotated(): return jnp.concatenate([parts[start:], parts[:start]], axis=0)]
    dot_general x4, matrix products: 3.16 us -> 1.75 us  [row_partials(): jnp.einsum('kpc,cb->kpb', weights.reshape(num_dp, rows // num_dp, cols),...]
where the time goes in v6:
time: 130 us
  blocking collectives  82.9 us (64%)
  starting transfers between devices  25.6 us (20%)
  waiting for transfers between devices  6.25 us (5%)
  other arithmetic  5.69 us (4%)
  matrix products  4.66 us (4%)
  local copies, waits for them, and re-layouts  3.62 us (3%)
    all_to_all x6, blocking collectives, exchange(): lax.all_to_all(parts, axis, 0, 0, axis_index_groups=[order], tiled=True)  82.9 us
    all_to_all x2, starting transfers between devices, exchange(): lax.all_to_all(parts, axis, 0, 0, axis_index_groups=[order], tiled=True)  25.6 us
    all_to_all x2, waiting for transfers between devices, exchange(): lax.all_to_all(parts, axis, 0, 0, axis_index_groups=[order], tiled=True)  6.25 us
  transfers between devices with their start and end apart: 2, of which 2 were waited for; matrix products, arithmetic and copies ran while one was open for 5% of the time, Pallas kernels for 0%

profile of v6, /device:TPU:1, one launch (start us, length us, event | category | flops | bytes accessed | tf_op | source)
XLA Modules:
  0.0 129.8 jit_solution(14331213394906548194)
XLA Ops:
  0.6 0.0 copy-start
  0.6 1.3 slice.117
  1.9 0.2 copy-done
  2.1 0.0 copy-start.3
  2.1 0.7 convolution_convert_fusion
  2.9 0.0 copy-done.3
  3.0 0.1 pad_maximum_fusion
  3.0 18.7 %all_to_all.40 = bf16[16,4,32,128]{3,2,1,0:T(8,128)(2,1)S(1)} all-to-all(bf16[16,4,32,128]{3,2,1,0:T(8,128)(2,1)S(1)} %pad_maximum_fusion), channel_id=1, replica_groups={{352,384,416,448,480,0,32,64,96,128,160,192,224,256,288,320},{353,385,4..., dimensions={0} | all-to-all | bytes 1048576 | tf_op jit(solution)/shard_map/all_to_all | solution.py:23
  21.8 0.0 copy-start.1
  21.8 0.0 copy-start.2
  21.8 0.0 copy-start.10
  21.8 0.0 copy-start.11
  21.8 0.0 copy-start.12
  21.8 0.0 copy-start.13
  21.8 0.0 copy-start.14
  21.8 0.0 copy-start.15
  21.9 0.0 copy-start.16
  21.9 0.4 fusion
  22.3 0.7 pad_maximum_fusion.1
  23.1 13.2 %all-to-all-start.1 = ((bf16[32,32,128]{2,1,0:T(8,128)(2,1)}), bf16[32,32,128]{2,1,0:T(8,128)(2,1)S(1)}, u32[]{:S(2)}, u32[]{:S(2)}) async-start(bf16[32,32,128]{2,1,0:T(8,128)(2,1)} %pad_maximum_fusion.1), calls=%async_computation.1 | async-start | bytes 524288 | tf_op jit(solution)/shard_map/all_to_all | solution.py:23
  36.3 0.8 dynamic-slice_convert_fusion
  37.1 0.1 convert_reduce_fusion
  37.1 5.4 %all-to-all-done.1 = bf16[32,32,128]{2,1,0:T(8,128)(2,1)S(1)} async-done(((bf16[32,32,128]{2,1,0:T(8,128)(2,1)}), bf16[32,32,128]{2,1,0:T(8,128)(2,1)S(1)}, u32[]{:S(2)}, u32[]{:S(2)}) %all-to-all-start.1) | async-done | bytes 262176 | tf_op jit(solution)/shard_map/all_to_all | solution.py:23
  42.6 0.0 copy-done.1
  42.6 0.0 copy-done.2
  42.6 0.0 copy-done.10
  42.7 0.0 copy-done.11
  42.7 0.0 copy-done.12
  42.7 0.0 copy-done.13
  42.7 0.0 copy-done.14
  42.7 0.0 copy-done.15
  42.7 0.0 copy-done.16
  42.7 0.1 fusion.44
  42.9 9.6 %all_to_all.41 = bf16[16,32,128]{2,1,0:T(8,128)(2,1)S(1)} all-to-all(bf16[16,32,128]{2,1,0:T(8,128)(2,1)S(1)} %broadcast_in_dim.17), channel_id=1, replica_groups={{352,384,416,448,480,0,32,64,96,128,160,192,224,256,288,320},{353,385,4..., dimensions={0} | all-to-all | bytes 262144 | tf_op jit(solution)/shard_map/all_to_all | solution.py:23
  52.5 0.0 copy-start.4
  52.5 0.4 fusion.1
  53.0 17.9 %all_to_all.42 = bf16[32,32,128]{2,1,0:T(8,128)(2,1)S(1)} all-to-all(bf16[32,32,128]{2,1,0:T(8,128)(2,1)S(1)} %pad_maximum_fusion.2), channel_id=1, replica_groups={{20,21,22,23,24,25,26,27,28,29,30,31,0,1,2,3,4,5,6,7,8,9,10,11,12,13,14..., dimensions={0} | all-to-all | bytes 524288 | tf_op jit(solution)/shard_map/all_to_all | solution.py:23
  71.0 0.1 fusion.42
  71.1 9.4 %all_to_all.43 = bf16[16,32,128]{2,1,0:T(8,128)(2,1)S(1)} all-to-all(bf16[16,32,128]{2,1,0:T(8,128)(2,1)S(1)} %broadcast_in_dim.18), channel_id=1, replica_groups={{352,384,416,448,480,0,32,64,96,128,160,192,224,256,288,320},{353,385,4..., dimensions={0} | all-to-all | bytes 262144 | tf_op jit(solution)/shard_map/all_to_all | solution.py:23
  80.6 0.0 copy-start.5
  80.6 0.4 fusion.2
  81.1 17.9 %all_to_all.44 = bf16[32,32,128]{2,1,0:T(8,128)(2,1)S(1)} all-to-all(bf16[32,32,128]{2,1,0:T(8,128)(2,1)S(1)} %pad_maximum_fusion.3), channel_id=1, replica_groups={{20,21,22,23,24,25,26,27,28,29,30,31,0,1,2,3,4,5,6,7,8,9,10,11,12,13,14..., dimensions={0} | all-to-all | bytes 524288 | tf_op jit(solution)/shard_map/all_to_all | solution.py:23
  99.1 0.1 fusion.41
  99.2 9.4 %all_to_all.45 = bf16[16,32,128]{2,1,0:T(8,128)(2,1)S(1)} all-to-all(bf16[16,32,128]{2,1,0:T(8,128)(2,1)S(1)} %broadcast_in_dim.19), channel_id=1, replica_groups={{352,384,416,448,480,0,32,64,96,128,160,192,224,256,288,320},{353,385,4..., dimensions={0} | all-to-all | bytes 262144 | tf_op jit(solution)/shard_map/all_to_all | solution.py:23
  108.7 0.0 copy-start.6
  108.7 0.4 fusion.3
  109.2 0.7 pad_maximum_fusion.4
  109.9 0.0 copy-done.4
  109.9 12.3 %all-to-all-start.7 = ((bf16[32,32,128]{2,1,0:T(8,128)(2,1)}), bf16[32,32,128]{2,1,0:T(8,128)(2,1)S(1)}, u32[]{:S(2)}, u32[]{:S(2)}) async-start(bf16[32,32,128]{2,1,0:T(8,128)(2,1)} %pad_maximum_fusion.4), calls=%async_computation.7 | async-start | bytes 524288 | tf_op jit(solution)/shard_map/all_to_all | solution.py:23
  122.2 0.7 broadcast_multiply_fusion
  122.9 0.7 multiply_subtract_fusion.1
  123.6 0.7 multiply_add_fusion.2
  124.3 0.0 copy-done.5
  124.3 0.0 copy-done.6
  124.3 2.2 %convolution_bitcast_fusion = f32[1024,512]{0,1:T(8,128)S(1)} fusion(bf16[4,1024,128]{2,1,0:T(8,128)(2,1)} %param.12, bf16[1,512,128]{2,1,0:T(8,128)(2,1)S(1)} %bitcast.215, bf16[1,512,128]{2,1,0:T(8,128)(2,1)} %bitcast.217, bf16[1,512,128]{2,1,0:T(8,128)(2,1)} %bitcast.219, bf16[1,512,128]{2,1,0:T(8,128)(2,1)} %bitcast.221), kind=kOutput, calls=%fused_computation | convolution fusion | flops 537657344 | bytes 3670016 | tf_op jit(solution)/shard_map/tpb,tcb->pc/dot_general | solution.py:130
  126.5 0.0 copy-start.7
  126.5 0.0 copy-start.8
  126.5 0.0 copy-start.9
  126.5 1.8 %copy.19 = f32[1024,512]{1,0:T(8,128)} copy(f32[1024,512]{0,1:T(8,128)S(1)} %convolution_bitcast_fusion) | data formatting | bytes 4194304
  128.3 0.8 all-to-all-done.7
  129.2 0.0 copy-done.7
  129.2 0.0 copy-done.8
  129.2 0.0 copy-done.9
  129.2 0.6 multiply_subtract_fusion
  (34 shorter events, 0.6 us)
Async XLA Ops:
  0.6 1.5 %copy-start = (bf16[1024,512]{1,0:T(8,128)(2,1)S(1)}, bf16[1024,512]{1,0:T(8,128)(2,1)}, u32[]{:S(2)}) copy-start(bf16[1024,512]{1,0:T(8,128)(2,1)} %param.13) | copy-start | bytes 3145732
  2.1 0.8 copy-start.3
  21.8 20.9 %copy-start.1 = (f32[32,128]{1,0:T(8,128)S(1)}, f32[32,128]{1,0:T(8,128)}, u32[]{:S(2)}) copy-start(f32[32,128]{1,0:T(8,128)} %param.16) | copy-start | bytes 49156
  21.8 20.9 %copy-start.2 = (f32[4,32,128]{2,1,0:T(8,128)S(1)}, f32[4,32,128]{2,1,0:T(8,128)}, u32[]{:S(2)}) copy-start(f32[4,32,128]{2,1,0:T(8,128)} %param.21) | copy-start | bytes 196612
  21.8 20.9 %copy-start.10 = (f32[4,32,128]{2,1,0:T(8,128)S(1)}, f32[4,32,128]{2,1,0:T(8,128)}, u32[]{:S(2)}) copy-start(f32[4,32,128]{2,1,0:T(8,128)} %param.14) | copy-start | bytes 196612
  21.8 20.9 %copy-start.11 = (f32[32,128]{1,0:T(8,128)S(1)}, f32[32,128]{1,0:T(8,128)}, u32[]{:S(2)}) copy-start(f32[32,128]{1,0:T(8,128)} %param.23) | copy-start | bytes 49156
  21.8 20.9 %copy-start.12 = (f32[32,128]{1,0:T(8,128)S(1)}, f32[32,128]{1,0:T(8,128)}, u32[]{:S(2)}) copy-start(f32[32,128]{1,0:T(8,128)} %param.15) | copy-start | bytes 49156
  21.8 20.9 %copy-start.13 = (f32[32]{0:T(128)S(1)}, f32[32]{0:T(128)}, u32[]{:S(2)}) copy-start(f32[32]{0:T(128)} %param.19) | copy-start | bytes 388
  21.8 20.9 %copy-start.14 = (f32[32]{0:T(128)S(1)}, f32[32]{0:T(128)}, u32[]{:S(2)}) copy-start(f32[32]{0:T(128)} %param.20) | copy-start | bytes 388
  21.8 20.9 %copy-start.15 = (f32[32]{0:T(128)S(1)}, f32[32]{0:T(128)}, u32[]{:S(2)}) copy-start(f32[32]{0:T(128)} %param.18) | copy-start | bytes 388
  21.9 20.9 %copy-start.16 = (f32[32]{0:T(128)S(1)}, f32[32]{0:T(128)}, u32[]{:S(2)}) copy-start(f32[32]{0:T(128)} %param.17) | copy-start | bytes 388
  23.1 19.5 %all-to-all-start.1 = ((bf16[32,32,128]{2,1,0:T(8,128)(2,1)}), bf16[32,32,128]{2,1,0:T(8,128)(2,1)S(1)}, u32[]{:S(2)}, u32[]{:S(2)}) async-start(bf16[32,32,128]{2,1,0:T(8,128)(2,1)} %pad_maximum_fusion.1), calls=%async_computation.1 | async-start | bytes 524288 | tf_op jit(solution)/shard_map/all_to_all | solution.py:23
  52.5 57.4 %copy-start.4 = (bf16[16,32,128]{2,1,0:T(8,128)(2,1)}, bf16[16,32,128]{2,1,0:T(8,128)(2,1)S(1)}, u32[]{:S(2)}) copy-start(bf16[16,32,128]{2,1,0:T(8,128)(2,1)S(1)} %pad_maximum_fusion.6) | copy-start | bytes 393220
  80.6 43.7 %copy-start.5 = (bf16[16,32,128]{2,1,0:T(8,128)(2,1)}, bf16[16,32,128]{2,1,0:T(8,128)(2,1)S(1)}, u32[]{:S(2)}) copy-start(bf16[16,32,128]{2,1,0:T(8,128)(2,1)S(1)} %pad_maximum_fusion.7) | copy-start | bytes 393220
  108.7 15.6 %copy-start.6 = (bf16[16,32,128]{2,1,0:T(8,128)(2,1)}, bf16[16,32,128]{2,1,0:T(8,128)(2,1)S(1)}, u32[]{:S(2)}) copy-start(bf16[16,32,128]{2,1,0:T(8,128)(2,1)S(1)} %pad_maximum_fusion.8) | copy-start | bytes 393220
  109.9 19.3 %all-to-all-start.7 = ((bf16[32,32,128]{2,1,0:T(8,128)(2,1)}), bf16[32,32,128]{2,1,0:T(8,128)(2,1)S(1)}, u32[]{:S(2)}, u32[]{:S(2)}) async-start(bf16[32,32,128]{2,1,0:T(8,128)(2,1)} %pad_maximum_fusion.4), calls=%async_computation.7 | async-start | bytes 524288 | tf_op jit(solution)/shard_map/all_to_all | solution.py:23
  126.5 2.7 %copy-start.7 = (f32[32,128]{1,0:T(8,128)S(1)}, f32[32,128]{1,0:T(8,128)}, u32[]{:S(2)}) copy-start(f32[32,128]{1,0:T(8,128)} %get-tuple-element.19) | copy-start | bytes 49156
  126.5 2.7 %copy-start.8 = (f32[32,128]{1,0:T(8,128)S(1)}, f32[32,128]{1,0:T(8,128)}, u32[]{:S(2)}) copy-start(f32[32,128]{1,0:T(8,128)} %multiply_add_fusion.2) | copy-start | bytes 49156
  126.5 2.7 %copy-start.9 = (f32[32,128]{1,0:T(8,128)S(1)}, f32[32,128]{1,0:T(8,128)}, u32[]{:S(2)}) copy-start(f32[32,128]{1,0:T(8,128)} %get-tuple-element.20) | copy-start | bytes 49156

commit v7 on v6

--- a/solution.py
+++ b/solution.py
@@ -128,8 +128,11 @@
             pieces = by_member(exchange(copies, "blk"), "blk")
             pieces = pieces.reshape(num_blk * own, trials)
     weight_sum = jnp.einsum(
-        "tpb,tcb->pc", spikes, jnp.stack(kept_pieces), preferred_element_type=f32
-    )
+        "tkpb,tcb->kpc",
+        spikes.reshape(num_steps, num_dp, -1, trials),
+        jnp.stack(kept_pieces),
+        preferred_element_type=f32,
+    ).reshape(rec_weights.shape)
     return (volt_adj, adapt_adj, weight_sum)
 
 

time: 130 us -> 130 us (level)
  waiting for transfers between devices: 6.25 us -> 10.8 us
  other arithmetic: 5.69 us -> 3.11 us
  local copies, waits for them, and re-layouts: 3.62 us -> 1.78 us
    all_to_all x2, waiting for transfers between devices: 6.25 us -> 10.8 us  [exchange(): lax.all_to_all(parts, axis, 0, 0, axis_index_groups=[order], tiled=True)]
    unnamed x35 -> x24, local copies, waits for them, and re-layouts: 2.09 us -> 0.25 us
  transfers between devices with their start and end apart: 2 -> 2, of which waited for: 2 -> 2; matrix products, arithmetic and copies ran while one was open for 5% -> 2% of each run, Pallas kernels for 0% -> 0%
where the time goes in v7:
time: 130 us
  blocking collectives  82.9 us (64%)
  starting transfers between devices  25.5 us (20%)
  waiting for transfers between devices  10.8 us (8%)
  matrix products  4.55 us (4%)
  other arithmetic  3.11 us (2%)
  local copies, waits for them, and re-layouts  1.78 us (1%)
    all_to_all x6, blocking collectives, exchange(): lax.all_to_all(parts, axis, 0, 0, axis_index_groups=[order], tiled=True)  82.9 us
    all_to_all x2, starting transfers between devices, exchange(): lax.all_to_all(parts, axis, 0, 0, axis_index_groups=[order], tiled=True)  25.5 us
    all_to_all x2, waiting for transfers between devices, exchange(): lax.all_to_all(parts, axis, 0, 0, axis_index_groups=[order], tiled=True)  10.8 us
  transfers between devices with their start and end apart: 2, of which 2 were waited for; matrix products, arithmetic and copies ran while one was open for 2% of the time, Pallas kernels for 0%

profile of v7, /device:TPU:1, one launch (start us, length us, event | category | flops | bytes accessed | tf_op | source)
XLA Modules:
  0.0 129.8 jit_solution(2577303655690285626)
XLA Ops:
  0.6 0.0 copy-start
  0.6 1.3 slice.117
  1.9 0.2 copy-done
  2.1 0.0 copy-start.4
  2.1 0.7 convolution_convert_fusion
  2.9 0.0 copy-done.4
  3.0 0.1 pad_maximum_fusion
  3.0 18.7 %all_to_all.40 = bf16[16,4,32,128]{3,2,1,0:T(8,128)(2,1)S(1)} all-to-all(bf16[16,4,32,128]{3,2,1,0:T(8,128)(2,1)S(1)} %pad_maximum_fusion), channel_id=1, replica_groups={{352,384,416,448,480,0,32,64,96,128,160,192,224,256,288,320},{353,385,4..., dimensions={0} | all-to-all | bytes 1048576 | tf_op jit(solution)/shard_map/all_to_all | solution.py:23
  21.7 0.0 copy-start.1
  21.8 0.0 copy-start.2
  21.8 0.0 copy-start.3
  21.8 0.0 copy-start.5
  21.8 0.0 copy-start.6
  21.8 0.0 copy-start.7
  21.8 0.0 copy-start.8
  21.8 0.0 copy-start.9
  21.8 0.0 copy-start.10
  21.9 0.0 copy-start.11
  21.9 0.4 fusion
  22.3 0.7 pad_maximum_fusion.1
  23.1 13.2 %all-to-all-start.1 = ((bf16[32,32,128]{2,1,0:T(8,128)(2,1)}), bf16[32,32,128]{2,1,0:T(8,128)(2,1)S(1)}, u32[]{:S(2)}, u32[]{:S(2)}) async-start(bf16[32,32,128]{2,1,0:T(8,128)(2,1)} %pad_maximum_fusion.1), calls=%async_computation.1 | async-start | bytes 524288 | tf_op jit(solution)/shard_map/all_to_all | solution.py:23
  36.3 0.0 copy-done.1
  36.3 0.1 convert_reduce_fusion
  36.4 6.2 %all-to-all-done.1 = bf16[32,32,128]{2,1,0:T(8,128)(2,1)S(1)} async-done(((bf16[32,32,128]{2,1,0:T(8,128)(2,1)}), bf16[32,32,128]{2,1,0:T(8,128)(2,1)S(1)}, u32[]{:S(2)}, u32[]{:S(2)}) %all-to-all-start.1) | async-done | bytes 262176 | tf_op jit(solution)/shard_map/all_to_all | solution.py:23
  42.6 0.0 copy-done.2
  42.6 0.0 copy-done.3
  42.7 0.0 copy-done.5
  42.7 0.0 copy-done.6
  42.7 0.0 copy-done.7
  42.7 0.0 copy-done.8
  42.7 0.0 copy-done.9
  42.7 0.0 copy-done.10
  42.7 0.0 copy-done.11
  42.7 0.1 fusion.46
  42.9 9.5 %all_to_all.41 = bf16[16,32,128]{2,1,0:T(8,128)(2,1)S(1)} all-to-all(bf16[16,32,128]{2,1,0:T(8,128)(2,1)S(1)} %broadcast_in_dim.17), channel_id=1, replica_groups={{352,384,416,448,480,0,32,64,96,128,160,192,224,256,288,320},{353,385,4..., dimensions={0} | all-to-all | bytes 262144 | tf_op jit(solution)/shard_map/all_to_all | solution.py:23
  52.5 0.4 fusion.1
  53.0 17.9 %all_to_all.42 = bf16[32,32,128]{2,1,0:T(8,128)(2,1)S(1)} all-to-all(bf16[32,32,128]{2,1,0:T(8,128)(2,1)S(1)} %pad_maximum_fusion.2), channel_id=1, replica_groups={{20,21,22,23,24,25,26,27,28,29,30,31,0,1,2,3,4,5,6,7,8,9,10,11,12,13,14..., dimensions={0} | all-to-all | bytes 524288 | tf_op jit(solution)/shard_map/all_to_all | solution.py:23
  71.0 0.1 fusion.44
  71.1 9.4 %all_to_all.43 = bf16[16,32,128]{2,1,0:T(8,128)(2,1)S(1)} all-to-all(bf16[16,32,128]{2,1,0:T(8,128)(2,1)S(1)} %broadcast_in_dim.18), channel_id=1, replica_groups={{352,384,416,448,480,0,32,64,96,128,160,192,224,256,288,320},{353,385,4..., dimensions={0} | all-to-all | bytes 262144 | tf_op jit(solution)/shard_map/all_to_all | solution.py:23
  80.6 0.4 fusion.2
  81.1 17.9 %all_to_all.44 = bf16[32,32,128]{2,1,0:T(8,128)(2,1)S(1)} all-to-all(bf16[32,32,128]{2,1,0:T(8,128)(2,1)S(1)} %pad_maximum_fusion.3), channel_id=1, replica_groups={{20,21,22,23,24,25,26,27,28,29,30,31,0,1,2,3,4,5,6,7,8,9,10,11,12,13,14..., dimensions={0} | all-to-all | bytes 524288 | tf_op jit(solution)/shard_map/all_to_all | solution.py:23
  99.1 0.1 fusion.43
  99.2 9.4 %all_to_all.45 = bf16[16,32,128]{2,1,0:T(8,128)(2,1)S(1)} all-to-all(bf16[16,32,128]{2,1,0:T(8,128)(2,1)S(1)} %broadcast_in_dim.19), channel_id=1, replica_groups={{352,384,416,448,480,0,32,64,96,128,160,192,224,256,288,320},{353,385,4..., dimensions={0} | all-to-all | bytes 262144 | tf_op jit(solution)/shard_map/all_to_all | solution.py:23
  108.7 0.4 fusion.3
  109.1 0.7 pad_maximum_fusion.4
  109.9 12.3 %all-to-all-start.7 = ((bf16[32,32,128]{2,1,0:T(8,128)(2,1)}), bf16[32,32,128]{2,1,0:T(8,128)(2,1)S(1)}, u32[]{:S(2)}, u32[]{:S(2)}) async-start(bf16[32,32,128]{2,1,0:T(8,128)(2,1)} %pad_maximum_fusion.4), calls=%async_computation.7 | async-start | bytes 524288 | tf_op jit(solution)/shard_map/all_to_all | solution.py:23
  122.2 0.1 broadcast_multiply_fusion
  122.2 0.1 multiply_subtract_fusion.1
  122.4 0.1 multiply_add_fusion.2
  122.4 2.1 %fusion.5 = f32[512,32,32,1]{0,2,1,3:T(8,128)} fusion(bf16[4,32,32,128]{3,2,1,0:T(8,128)(2,1)S(1)} %bitcast.223, bf16[1,512,128]{2,1,0:T(8,128)(2,1)S(1)} %bitcast.226, bf16[1,512,128]{2,1,0:T(8,128)(2,1)S(1)} %bitcast.228, bf16[1,512,128]{2,1,0:T(8,128)(2,1)S(1)} %bitcast.230, bf16[1,512,128]{2,1,0:T(8,128)(2,1)S(1)} %bitcast.232), kind=kOutput, calls=%fused_computation.11 | convolution fusion | flops 538968064 | bytes 3670016 | tf_op jit(solution)/shard_map/tkpb,tcb->kpc/dot_general | solution.py:130
  124.5 4.6 %all-to-all-done.7 = bf16[32,32,128]{2,1,0:T(8,128)(2,1)S(1)} async-done(((bf16[32,32,128]{2,1,0:T(8,128)(2,1)}), bf16[32,32,128]{2,1,0:T(8,128)(2,1)S(1)}, u32[]{:S(2)}, u32[]{:S(2)}) %all-to-all-start.7) | async-done | bytes 262176 | tf_op jit(solution)/shard_map/all_to_all | solution.py:23
  129.1 0.6 multiply_subtract_fusion
  (35 shorter events, 0.6 us)
Async XLA Ops:
  0.6 1.5 %copy-start = (bf16[1024,512]{1,0:T(8,128)(2,1)S(1)}, bf16[1024,512]{1,0:T(8,128)(2,1)}, u32[]{:S(2)}) copy-start(bf16[1024,512]{1,0:T(8,128)(2,1)} %param.13) | copy-start | bytes 3145732
  2.1 0.8 copy-start.4
  21.7 14.6 %copy-start.1 = (bf16[4,1024,128]{2,1,0:T(8,128)(2,1)S(1)}, bf16[4,1024,128]{2,1,0:T(8,128)(2,1)}, u32[]{:S(2)}) copy-start(bf16[4,1024,128]{2,1,0:T(8,128)(2,1)} %param.12) | copy-start | bytes 3145732
  21.8 20.9 %copy-start.2 = (f32[32,128]{1,0:T(8,128)S(1)}, f32[32,128]{1,0:T(8,128)}, u32[]{:S(2)}) copy-start(f32[32,128]{1,0:T(8,128)} %param.16) | copy-start | bytes 49156
  21.8 20.9 %copy-start.3 = (f32[4,32,128]{2,1,0:T(8,128)S(1)}, f32[4,32,128]{2,1,0:T(8,128)}, u32[]{:S(2)}) copy-start(f32[4,32,128]{2,1,0:T(8,128)} %param.21) | copy-start | bytes 196612
  21.8 20.9 %copy-start.5 = (f32[4,32,128]{2,1,0:T(8,128)S(1)}, f32[4,32,128]{2,1,0:T(8,128)}, u32[]{:S(2)}) copy-start(f32[4,32,128]{2,1,0:T(8,128)} %param.14) | copy-start | bytes 196612
  21.8 20.9 %copy-start.6 = (f32[32,128]{1,0:T(8,128)S(1)}, f32[32,128]{1,0:T(8,128)}, u32[]{:S(2)}) copy-start(f32[32,128]{1,0:T(8,128)} %param.23) | copy-start | bytes 49156
  21.8 20.9 %copy-start.7 = (f32[32,128]{1,0:T(8,128)S(1)}, f32[32,128]{1,0:T(8,128)}, u32[]{:S(2)}) copy-start(f32[32,128]{1,0:T(8,128)} %param.15) | copy-start | bytes 49156
  21.8 20.9 %copy-start.8 = (f32[32]{0:T(128)S(1)}, f32[32]{0:T(128)}, u32[]{:S(2)}) copy-start(f32[32]{0:T(128)} %param.19) | copy-start | bytes 388
  21.8 20.9 %copy-start.9 = (f32[32]{0:T(128)S(1)}, f32[32]{0:T(128)}, u32[]{:S(2)}) copy-start(f32[32]{0:T(128)} %param.20) | copy-start | bytes 388
  21.8 20.9 %copy-start.10 = (f32[32]{0:T(128)S(1)}, f32[32]{0:T(128)}, u32[]{:S(2)}) copy-start(f32[32]{0:T(128)} %param.18) | copy-start | bytes 388
  21.9 20.9 %copy-start.11 = (f32[32]{0:T(128)S(1)}, f32[32]{0:T(128)}, u32[]{:S(2)}) copy-start(f32[32]{0:T(128)} %param.17) | copy-start | bytes 388
  23.1 19.5 %all-to-all-start.1 = ((bf16[32,32,128]{2,1,0:T(8,128)(2,1)}), bf16[32,32,128]{2,1,0:T(8,128)(2,1)S(1)}, u32[]{:S(2)}, u32[]{:S(2)}) async-start(bf16[32,32,128]{2,1,0:T(8,128)(2,1)} %pad_maximum_fusion.1), calls=%async_computation.1 | async-start | bytes 524288 | tf_op jit(solution)/shard_map/all_to_all | solution.py:23
  109.9 19.2 %all-to-all-start.7 = ((bf16[32,32,128]{2,1,0:T(8,128)(2,1)}), bf16[32,32,128]{2,1,0:T(8,128)(2,1)S(1)}, u32[]{:S(2)}, u32[]{:S(2)}) async-start(bf16[32,32,128]{2,1,0:T(8,128)(2,1)} %pad_maximum_fusion.4), calls=%async_computation.7 | async-start | bytes 524288 | tf_op jit(solution)/shard_map/all_to_all | solution.py:23

commit v8 on v7

--- a/solution.py
+++ b/solution.py
@@ -9,8 +9,7 @@
 
 
 def leader(axis):
-    size = lax.axis_size(axis)
-    return size * 5 // 8 if axis == "dp" else size * 11 // 16
+    return lax.axis_size(axis) * 5 // 8
 
 
 def rotated(parts, start):
@@ -56,9 +55,6 @@
     own, trials = volt_init.shape
     num_blk = lax.axis_size("blk")
     num_dp = lax.axis_size("dp")
-    own_fired = lax.dynamic_slice_in_dim(
-        spikes, lax.axis_index("dp") * own, own, 1
-    ).astype(f32)
     leak_rate = mem_decay[:, None]
     keep_rate = adapt_decay[:, None]
     gain_col = adapt_gain[:, None]
@@ -68,11 +64,17 @@
     sums = jnp.einsum(
         "pc,tpb->ctb", rec_weights, early, preferred_element_type=f32
     ).astype(bf16)
-    sums, last_adj = lax.optimization_barrier((sums, volt_cot))
+    sums, last_adj, own_start = lax.optimization_barrier(
+        (sums, volt_cot, lax.axis_index("dp") * own)
+    )
     sums = sums.reshape(num_blk, own, num_steps - 1, trials).swapaxes(1, 2)
     sums = rotated(sums, leader("blk"))
     copies = jnp.broadcast_to(last_adj.astype(bf16), (num_blk, 1, own, trials))
     arrived = exchange(jnp.concatenate([sums, copies], axis=1), "blk")
+    arrived, late_spikes = lax.optimization_barrier((arrived, spikes))
+    own_fired = lax.dynamic_slice_in_dim(
+        late_spikes, own_start, own, 1, allow_negative_indices=False
+    ).astype(f32)
     currents = jnp.sum(arrived[:, : num_steps - 1].astype(f32), axis=0)
     pieces = by_member(arrived[:, num_steps - 1], "blk").reshape(num_blk * own, trials)
 
@@ -99,6 +101,10 @@
     volt_adj = volt_cot
     adapt_adj = adapt_cot
     kept_pieces = []
+    outgoing = row_partials(rec_weights, pieces, num_dp)
+    outgoing, surrogates, threshold_values, own_fired = lax.optimization_barrier(
+        (outgoing, surrogates, threshold_values, own_fired)
+    )
     for t in reversed(range(num_steps)):
         if t == 0:
             pieces, first_volt, first_adapt = lax.optimization_barrier(
@@ -107,7 +113,9 @@
             thresh = threshold(first_adapt)
             surrogate = surrogate_of(first_volt, thresh)
         kept_pieces.insert(0, pieces)
-        partials = exchange(row_partials(rec_weights, pieces, num_dp), "dp")
+        if t + 1 < num_steps:
+            outgoing = row_partials(rec_weights, pieces, num_dp)
+        partials = exchange(outgoing, "dp")
         if t > 0:
             thresh, surrogate = threshold_values[t], surrogates[t]
         known = pulse_sensitivity[t] - thresh * volt_adj + adapt_adj
@@ -129,7 +137,7 @@
             pieces = pieces.reshape(num_blk * own, trials)
     weight_sum = jnp.einsum(
         "tkpb,tcb->kpc",
-        spikes.reshape(num_steps, num_dp, -1, trials),
+        late_spikes.reshape(num_steps, num_dp, -1, trials),
         jnp.stack(kept_pieces),
         preferred_element_type=f32,
     ).reshape(rec_weights.shape)

time: 130 us -> 131 us (level)
  blocking collectives: 82.9 us -> 104 us
  starting transfers between devices: 25.5 us -> 12.4 us
  waiting for transfers between devices: 10.8 us -> 4.6 us
    all_to_all x6 -> x7, blocking collectives: 82.9 us -> 104 us  [exchange(): lax.all_to_all(parts, axis, 0, 0, axis_index_groups=[order], tiled=True)]
    all_to_all x2 -> x1, starting transfers between devices: 25.5 us -> 12.4 us  [exchange(): lax.all_to_all(parts, axis, 0, 0, axis_index_groups=[order], tiled=True)]
    all_to_all x2 -> x1, waiting for transfers between devices: 10.8 us -> 4.6 us  [exchange(): lax.all_to_all(parts, axis, 0, 0, axis_index_groups=[order], tiled=True)]
  transfers between devices with their start and end apart: 2 -> 1, of which waited for: 2 -> 1; matrix products, arithmetic and copies ran while one was open for 2% -> 2% of each run, Pallas kernels for 0% -> 0%
where the time goes in v8:
time: 131 us
  blocking collectives  104 us (79%)
  starting transfers between devices  12.4 us (9%)
  waiting for transfers between devices  4.6 us (4%)
  matrix products  4.55 us (3%)
  other arithmetic  2.47 us (2%)
  local copies, waits for them, and re-layouts  1.88 us (1%)
    all_to_all x7, blocking collectives, exchange(): lax.all_to_all(parts, axis, 0, 0, axis_index_groups=[order], tiled=True)  104 us
    all_to_all x1, starting transfers between devices, exchange(): lax.all_to_all(parts, axis, 0, 0, axis_index_groups=[order], tiled=True)  12.4 us
    all_to_all x1, waiting for transfers between devices, exchange(): lax.all_to_all(parts, axis, 0, 0, axis_index_groups=[order], tiled=True)  4.6 us
  transfers between devices with their start and end apart: 1, of which 1 were waited for; matrix products, arithmetic and copies ran while one was open for 2% of the time, Pallas kernels for 0%

profile of v8, /device:TPU:1, one launch (start us, length us, event | category | flops | bytes accessed | tf_op | source)
XLA Modules:
  0.0 130.8 jit_solution(11482354564667840348)
XLA Ops:
  0.6 0.0 copy-start
  0.6 1.3 slice.123
  1.9 0.2 copy-done
  2.1 0.0 copy-start.4
  2.1 0.7 convolution_convert_fusion
  2.9 0.0 copy-done.4
  3.0 0.1 pad_maximum_fusion
  3.0 0.0 copy-start.1
  3.1 19.1 %all_to_all.40 = bf16[16,4,32,128]{3,2,1,0:T(8,128)(2,1)S(1)} all-to-all(bf16[16,4,32,128]{3,2,1,0:T(8,128)(2,1)S(1)} %pad_maximum_fusion), channel_id=1, replica_groups={{320,352,384,416,448,480,0,32,64,96,128,160,192,224,256,288},{321,353,3..., dimensions={0} | all-to-all | bytes 1048576 | tf_op jit(solution)/shard_map/all_to_all | solution.py:22
  22.1 0.0 copy-start.2
  22.1 0.0 copy-start.5
  22.1 0.0 copy-start.7
  22.2 0.0 copy-start.8
  22.2 0.0 copy-start.9
  22.2 0.0 copy-start.10
  22.2 0.0 copy-start.11
  22.2 0.1 convert_reduce_fusion
  22.3 0.0 copy-start.3
  22.3 0.0 copy-start.6
  22.3 0.4 fusion
  22.8 0.0 copy-done.1
  22.9 0.0 copy-done.2
  22.9 0.0 copy-done.5
  22.9 0.1 copy-done.7
  23.0 0.0 copy-done.8
  23.0 0.0 copy-done.9
  23.0 0.0 copy-done.10
  23.0 0.0 copy-done.11
  23.0 0.1 fusion.21
  23.2 19.6 %all_to_all.41 = bf16[32,32,128]{2,1,0:T(8,128)(2,1)S(1)} all-to-all(bf16[32,32,128]{2,1,0:T(8,128)(2,1)S(1)} %pad_maximum_fusion.1), channel_id=1, replica_groups={{20,21,22,23,24,25,26,27,28,29,30,31,0,1,2,3,4,5,6,7,8,9,10,11,12,13,14..., dimensions={0} | all-to-all | bytes 524288 | tf_op jit(solution)/shard_map/all_to_all | solution.py:22
  42.8 0.0 copy-done.3
  42.9 0.0 copy-done.6
  42.9 0.1 fusion.57
  43.0 9.7 %all_to_all.42 = bf16[16,32,128]{2,1,0:T(8,128)(2,1)S(1)} all-to-all(bf16[16,32,128]{2,1,0:T(8,128)(2,1)S(1)} %broadcast_in_dim.17), channel_id=1, replica_groups={{320,352,384,416,448,480,0,32,64,96,128,160,192,224,256,288},{321,353,3..., dimensions={0} | all-to-all | bytes 262144 | tf_op jit(solution)/shard_map/all_to_all | solution.py:22
  52.7 0.4 fusion.1
  53.2 18.0 %all_to_all.43 = bf16[32,32,128]{2,1,0:T(8,128)(2,1)S(1)} all-to-all(bf16[32,32,128]{2,1,0:T(8,128)(2,1)S(1)} %pad_maximum_fusion.2), channel_id=1, replica_groups={{20,21,22,23,24,25,26,27,28,29,30,31,0,1,2,3,4,5,6,7,8,9,10,11,12,13,14..., dimensions={0} | all-to-all | bytes 524288 | tf_op jit(solution)/shard_map/all_to_all | solution.py:22
  71.2 0.1 fusion.55
  71.3 9.7 %all_to_all.44 = bf16[16,32,128]{2,1,0:T(8,128)(2,1)S(1)} all-to-all(bf16[16,32,128]{2,1,0:T(8,128)(2,1)S(1)} %broadcast_in_dim.18), channel_id=1, replica_groups={{320,352,384,416,448,480,0,32,64,96,128,160,192,224,256,288},{321,353,3..., dimensions={0} | all-to-all | bytes 262144 | tf_op jit(solution)/shard_map/all_to_all | solution.py:22
  81.1 0.4 fusion.2
  81.6 18.1 %all_to_all.45 = bf16[32,32,128]{2,1,0:T(8,128)(2,1)S(1)} all-to-all(bf16[32,32,128]{2,1,0:T(8,128)(2,1)S(1)} %pad_maximum_fusion.3), channel_id=1, replica_groups={{20,21,22,23,24,25,26,27,28,29,30,31,0,1,2,3,4,5,6,7,8,9,10,11,12,13,14..., dimensions={0} | all-to-all | bytes 524288 | tf_op jit(solution)/shard_map/all_to_all | solution.py:22
  99.7 0.1 fusion.53
  99.8 9.7 %all_to_all.46 = bf16[16,32,128]{2,1,0:T(8,128)(2,1)S(1)} all-to-all(bf16[16,32,128]{2,1,0:T(8,128)(2,1)S(1)} %broadcast_in_dim.19), channel_id=1, replica_groups={{320,352,384,416,448,480,0,32,64,96,128,160,192,224,256,288},{321,353,3..., dimensions={0} | all-to-all | bytes 262144 | tf_op jit(solution)/shard_map/all_to_all | solution.py:22
  109.6 0.4 fusion.3
  110.0 0.7 pad_maximum_fusion.4
  110.8 12.4 %all-to-all-start.7 = ((bf16[32,32,128]{2,1,0:T(8,128)(2,1)}), bf16[32,32,128]{2,1,0:T(8,128)(2,1)S(1)}, u32[]{:S(2)}, u32[]{:S(2)}) async-start(bf16[32,32,128]{2,1,0:T(8,128)(2,1)} %pad_maximum_fusion.4), calls=%async_computation.7 | async-start | bytes 524288 | tf_op jit(solution)/shard_map/all_to_all | solution.py:22
  123.2 0.1 broadcast_multiply_fusion
  123.3 0.1 fusion.30
  123.4 0.1 multiply_add_fusion.2
  123.5 2.1 %convolution_bitcast_fusion = f32[1024,512]{1,0:T(8,128)} fusion(bf16[4,1024,128]{2,1,0:T(8,128)(2,1)S(1)} %copy-done.1, bf16[1,512,128]{2,1,0:T(8,128)(2,1)S(1)} %bitcast.231, bf16[1,512,128]{2,1,0:T(8,128)(2,1)S(1)} %bitcast.233, bf16[1,512,128]{2,1,0:T(8,128)(2,1)S(1)} %bitcast.235, bf16[1,512,128]{2,1,0:T(8,128)(2,1)S(1)} %bitcast.237), kind=kOutput, calls=%fused_computation | convolution fusion | flops 537657344 | bytes 3670016 | tf_op jit(solution)/shard_map/tkpb,tcb->kpc/dot_general | solution.py:138
  125.6 4.6 %all-to-all-done.7 = bf16[32,32,128]{2,1,0:T(8,128)(2,1)S(1)} async-done(((bf16[32,32,128]{2,1,0:T(8,128)(2,1)}), bf16[32,32,128]{2,1,0:T(8,128)(2,1)S(1)}, u32[]{:S(2)}, u32[]{:S(2)}) %all-to-all-start.7) | async-done | bytes 262176 | tf_op jit(solution)/shard_map/all_to_all | solution.py:22
  130.2 0.6 multiply_subtract_fusion
  (37 shorter events, 0.6 us)
Async XLA Ops:
  0.6 1.5 %copy-start = (bf16[1024,512]{1,0:T(8,128)(2,1)S(1)}, bf16[1024,512]{1,0:T(8,128)(2,1)}, u32[]{:S(2)}) copy-start(bf16[1024,512]{1,0:T(8,128)(2,1)} %param.13) | copy-start | bytes 3145732
  2.1 0.8 copy-start.4
  3.0 19.8 %copy-start.1 = (bf16[4,1024,128]{2,1,0:T(8,128)(2,1)S(1)}, bf16[4,1024,128]{2,1,0:T(8,128)(2,1)}, u32[]{:S(2)}) copy-start(bf16[4,1024,128]{2,1,0:T(8,128)(2,1)} %param.12) | copy-start | bytes 3145732
  22.1 0.7 copy-start.2
  22.1 0.8 copy-start.5
  22.1 0.9 copy-start.7
  22.2 0.9 copy-start.8
  22.2 0.9 copy-start.9
  22.2 0.9 copy-start.10
  22.2 0.8 copy-start.11
  22.3 20.5 %copy-start.3 = (f32[4,32,128]{2,1,0:T(8,128)S(1)}, f32[4,32,128]{2,1,0:T(8,128)}, u32[]{:S(2)}) copy-start(f32[4,32,128]{2,1,0:T(8,128)} %param.21) | copy-start | bytes 196612
  22.3 20.5 %copy-start.6 = (f32[32,128]{1,0:T(8,128)S(1)}, f32[32,128]{1,0:T(8,128)}, u32[]{:S(2)}) copy-start(f32[32,128]{1,0:T(8,128)} %param.23) | copy-start | bytes 49156
  110.8 19.4 %all-to-all-start.7 = ((bf16[32,32,128]{2,1,0:T(8,128)(2,1)}), bf16[32,32,128]{2,1,0:T(8,128)(2,1)S(1)}, u32[]{:S(2)}, u32[]{:S(2)}) async-start(bf16[32,32,128]{2,1,0:T(8,128)(2,1)} %pad_maximum_fusion.4), calls=%async_computation.7 | async-start | bytes 524288 | tf_op jit(solution)/shard_map/all_to_all | solution.py:22
